TPU v7x, 256 devices: a whole 4x4x8 slice. The times are simulated.
256 devices in a mesh: box: 128 (over z, x, y), help: 2 (over core).
Axes of the slice: x: 4, y: 4, z: 8, core: 2. Of those that a mesh axis runs over, the one named last changes fastest.
Arguments:
- prim_pos: float32 [3, 16384], P(None, ('box', 'help')), may hold values from 0 to 1
- prim_weight: float32 [16384], P(('box', 'help')), may hold values from 0.3 to 3
- sec_pos: float32 [2048, 3, 128], P(('box', 'help')), may hold values from 0 to 1
- sec_weight: float32 [2048, 128], P(('box', 'help')), may hold values from 0.3 to 3
- sec_counts: int32 [2048], P(('box', 'help')), may hold values from 1 to 128, as said below
- tile_lists: int32 [1024, 12], P(('box', 'help')), may hold values from -1 to 2047, as said below
- region_of: int32 [16384, 1], P(('box', 'help')), may hold values from 0 to 255; in each aligned block of 64 rows (0 to 63, 64 to 127, ...) at most 2 rows name the same one
Outputs:
- coefficients: bfloat16 [16384, 1936], P(('box', 'help'))
- region_tensor: float32 [256, 129536], P(('box', 'help'))
Inputs may be any that keep to these rules, and one draw needn't show every extreme that they name: Block g holds sec_counts[g] live secondaries in its first slots; every device holds at least one block with all 128 slots live. `tile_lists`: row t lists distinct blocks for the primaries t * 16 to (t + 1) * 16 - 1. Every listed block belongs to a device whose box index is within one, cyclically, of the box index of the device that holds the tile, with any help index. Unused slots hold -1 and come after the used ones; at least 6 slots are used, and each device has a tile that uses all 12. `region_of`: within the rows of one device (aligned blocks of 64 rows) no region is named more than 2 times, a bound that some block reaches. Region r is owned by the device of index r along box+help.
All inputs are finite; a program needn't handle non-finite values.
Results may differ from a plain program's by a relative error of at most 0.0075.
Values may be sent and summed in bfloat16 or wider, within the bound.
A program may use at most 64 MiB of HBM per device.

v0:
```python
import functools
import math

import jax
import jax.numpy as jnp
from jax import lax
from jax.experimental import pallas as pl
from jax.experimental.pallas import tpu as pltpu
from jax.sharding import PartitionSpec as P

LMAX = 10
NBIN = 16
BS = 128
LIST = 12
PT = 16
PRIM_DEV = 64
NHARM = (LMAX + 1) ** 2
FEAT = NHARM * NBIN
WIDE = 2048

GROUPS = ((0, 1), (2, 3), (4, 5, 6), (7, 8, 9, 10))


def padded(cells, sides, width):
    for axis, dim in sides:
        count = lax.axis_size(axis)
        head = lax.slice_in_dim(cells, 0, width, axis=dim)
        tail = lax.slice_in_dim(cells, cells.shape[dim] - width, cells.shape[dim], axis=dim)
        cells = jnp.concatenate(
            [
                lax.ppermute(tail, axis, [(i, (i + 1) % count) for i in range(count)]),
                cells,
                lax.ppermute(head, axis, [((i + 1) % count, i) for i in range(count)]),
            ],
            axis=dim,
        )
    return cells


def order_slices(degree_top, bin_count):
    slices = []
    position = 0
    for m_order in range(degree_top + 1):
        length = (degree_top + 1 - m_order) * bin_count
        if m_order == 0:
            slices.append((position, -1, length))
            position = position + length
        else:
            slices.append((position, position + length, length))
            position = position + 2 * length
    return slices


def harmonic_scale(m_order, degree):
    factor = math.sqrt(
        (2 * degree + 1)
        / (4.0 * math.pi)
        * math.factorial(degree - m_order)
        / math.factorial(degree + m_order)
    )
    if m_order > 0:
        factor = factor * math.sqrt(2.0)
    lead = 1.0
    for odd_value in range(1, 2 * m_order, 2):
        lead = lead * odd_value
    for step in range(m_order + 1, degree + 1):
        lead = lead * (2 * step - 1) / (step - m_order)
    return factor * lead


def first_row(m_order):
    return order_slices(LMAX, 1)[m_order][0]


def pair_kernel(pick_ref, count_ref, pool_ref, prim_ref, coef_ref, packed, basis, spline, acc, diag, spread):
    tile = pl.program_id(0)
    lane = lax.broadcasted_iota(jnp.int32, (8, BS), 1)

    @pl.when(tile == 0)
    def _():
        row = lax.broadcasted_iota(jnp.int32, (PT * NBIN, 128), 0)
        col = lax.broadcasted_iota(jnp.int32, (PT * NBIN, 128), 1)
        for part in range(8):
            spread[part] = jnp.where(col == part * NBIN + row // PT, 1.0, 0.0).astype(jnp.bfloat16)

    packed[...] = jnp.zeros_like(packed)
    filled = jnp.int32(0)
    for slot in range(LIST):
        pick = pick_ref[tile, slot]
        block = pool_ref[jnp.maximum(pick, 0)]
        base = filled // BS
        shift = filled % BS
        moved = pltpu.roll(block, shift, 1)
        used = pick >= 0
        low = jnp.where((lane >= shift) & used, moved, packed[base])
        packed[base] = low
        high = jnp.where((lane < shift) & used, moved, packed[base + 1])
        packed[base + 1] = high
        filled = filled + jnp.where(used, count_ref[jnp.maximum(pick, 0)], 0)
    chunks = (filled + 2 * BS - 1) // (2 * BS)

    acc[...] = jnp.zeros_like(acc)
    prim = prim_ref[...]
    px, py, pz = prim[:, 0:1], prim[:, 1:2], prim[:, 2:3]
    bin_step = 1.0 / (NBIN + 1)

    def chunk_step(chunk, carry):
        geometry = []
        for half in range(2):
            rows = packed[2 * chunk + half]
            dx = rows[0:1, :] - px
            dy = rows[1:2, :] - py
            dz = rows[2:3, :] - pz
            weight = jnp.broadcast_to(rows[3:4, :], (PT, BS))
            radius = jnp.sqrt(dx * dx + dy * dy + dz * dz)
            inverse = 1.0 / jnp.maximum(radius, 0.5 * bin_step)
            geometry.append((dx * inverse, dy * inverse, dz * inverse))
            place = radius * float(NBIN + 1)
            whole = jnp.floor(place)
            part = place - whole
            upper = weight * part
            lower = weight * (1.0 - part)
            cols = slice(half * BS, (half + 1) * BS)
            above = jnp.where(whole == 0.0, upper, 0.0)
            for bin_at in range(NBIN):
                here = whole == float(bin_at + 1)
                spline[bin_at * PT : (bin_at + 1) * PT, cols] = jnp.where(here, lower, above).astype(
                    jnp.bfloat16
                )
                above = jnp.where(here, upper, 0.0)
        angular = [[None, None], [None, None]]
        for orders in GROUPS:
            for half in range(2):
                ux, uy, uz = geometry[half]
                cols = slice(half * BS, (half + 1) * BS)
                for m_order in orders:
                    if m_order == 1:
                        angular[half] = [ux, uy]
                    elif m_order > 1:
                        cos_part, sin_part = angular[half]
                        angular[half] = [
                            cos_part * ux - sin_part * uy,
                            sin_part * ux + cos_part * uy,
                        ]
                    older, newer = None, None
                    start = first_row(m_order)
                    count = LMAX + 1 - m_order
                    for degree in range(m_order, LMAX + 1):
                        if degree == m_order:
                            current = None
                        elif degree == m_order + 1:
                            current = uz
                        else:
                            ratio = (degree + m_order - 1) * (degree - m_order - 1) / (
                                (2 * degree - 1) * (2 * degree - 3)
                            )
                            if older is None:
                                current = uz * newer - ratio
                            else:
                                current = uz * newer - ratio * older
                        older, newer = newer, current
                        scale = harmonic_scale(m_order, degree)
                        at = (start + degree - m_order) * PT
                        if current is None:
                            scaled = None
                        else:
                            scaled = current * scale
                        if m_order == 0:
                            value = jnp.full((PT, BS), scale, jnp.float32) if scaled is None else scaled
                            basis[at : at + PT, cols] = value.astype(jnp.bfloat16)
                        else:
                            for kind in range(2):
                                turn = angular[half][kind]
                                value = turn * scale if scaled is None else scaled * turn
                                low = at + kind * count * PT
                                basis[low : low + PT, cols] = value.astype(jnp.bfloat16)
            first = first_row(orders[0]) * PT
            last = NHARM * PT if orders[-1] == LMAX else first_row(orders[-1] + 1) * PT
            acc[first:last, :] += lax.dot_general(
                basis[first:last, :],
                spline[...],
                (((1,), (1,)), ((), ())),
                preferred_element_type=jnp.float32,
            )
        return carry

    lax.fori_loop(0, chunks, chunk_step, 0)

    row = lax.broadcasted_iota(jnp.int32, (PT, PT * NBIN), 0)
    col = lax.broadcasted_iota(jnp.int32, (PT, PT * NBIN), 1)
    keep = jnp.where(col % PT == row, prim[:, 3:4], 0.0)
    for harm in range(128):
        if harm < NHARM:
            value = (acc[harm * PT : (harm + 1) * PT, :] * keep).astype(jnp.bfloat16)
        else:
            value = jnp.zeros((PT, PT * NBIN), jnp.bfloat16)
        diag[harm % 8, (harm // 8) * PT : (harm // 8 + 1) * PT, :] = value
    total = jnp.zeros((256, 128), jnp.float32)
    for part in range(8):
        total = total + jnp.dot(diag[part], spread[part], preferred_element_type=jnp.float32)
    rows = total.astype(jnp.bfloat16)
    for group in range(15):
        coef_ref[:, group * 128 : (group + 1) * 128] = rows[group * PT : (group + 1) * PT, :]
    coef_ref[:, 1920:FEAT] = rows[15 * PT : 16 * PT, : FEAT - 1920]


def pair_sums(pick, counts, pool, prim):
    tiles = pick.shape[0]
    return pl.pallas_call(
        pair_kernel,
        out_shape=jax.ShapeDtypeStruct((tiles * PT, FEAT), jnp.bfloat16),
        grid_spec=pltpu.PrefetchScalarGridSpec(
            num_scalar_prefetch=2,
            grid=(tiles,),
            in_specs=[
                pl.BlockSpec(pool.shape, lambda t, *_: (0, 0, 0)),
                pl.BlockSpec((PT, prim.shape[1]), lambda t, *_: (t, 0)),
            ],
            out_specs=pl.BlockSpec((PT, FEAT), lambda t, *_: (t, 0)),
            scratch_shapes=[
                pltpu.VMEM((2 * ((LIST + 1) // 2) + 2, 8, BS), jnp.float32),
                pltpu.VMEM((NHARM * PT, 2 * BS), jnp.bfloat16),
                pltpu.VMEM((NBIN * PT, 2 * BS), jnp.bfloat16),
                pltpu.VMEM((NHARM * PT, NBIN * PT), jnp.float32),
                pltpu.VMEM((8, 256, NBIN * PT), jnp.bfloat16),
                pltpu.VMEM((8, NBIN * PT, 128), jnp.bfloat16),
            ],
        ),
        compiler_params=pltpu.CompilerParams(vmem_limit_bytes=40 << 20),
        name="pair_sums",
    )(pick, counts, pool, prim)


def self_product(left_rows, right_rows):
    return lax.dot_general(
        left_rows, right_rows, (((0,), (0,)), ((), ())), preferred_element_type=jnp.float32
    )


def gram_by_order(owner_rows):
    pieces = []
    for cos_start, sin_start, length in order_slices(LMAX, NBIN):
        cos_rows = owner_rows[:, cos_start : cos_start + length]
        gram_block = self_product(cos_rows, cos_rows)
        if sin_start >= 0:
            sine_rows = owner_rows[:, sin_start : sin_start + length]
            gram_block = gram_block + self_product(sine_rows, sine_rows)
        pieces.append(gram_block.reshape(-1))
    return jnp.concatenate(pieces)


def shards(prim_pos, prim_weight, sec_pos, sec_weight, sec_counts, tile_lists, region_of):
    box_count = lax.axis_size("box")
    help_count = lax.axis_size("help")
    per_device = sec_pos.shape[0]
    lane_index = jnp.arange(sec_pos.shape[2], dtype=jnp.int32)
    live_mask = (lane_index[None, :] < sec_counts[:, None]).astype(jnp.float32)
    count_row = jnp.broadcast_to(
        sec_counts.astype(jnp.float32)[:, None, None], (per_device, 4, sec_pos.shape[2])
    )
    own_blocks = jnp.concatenate(
        [sec_pos, (sec_weight * live_mask)[:, None, :], count_row], axis=1
    )
    chip_pool = lax.all_gather(own_blocks, "help", axis=0, tiled=True)
    block_pool = padded(chip_pool, (("box", 0),), chip_pool.shape[0])
    pool_counts = block_pool[:, 4, 0].astype(jnp.int32)
    in_use = tile_lists >= 0
    safe_list = jnp.where(in_use, tile_lists, 0)
    owner_dev = safe_list // per_device
    box_move = jnp.mod(owner_dev // help_count - lax.axis_index("box") + 1, box_count)
    pool_index = (
        box_move * (help_count * per_device)
        + owner_dev % help_count * per_device
        + safe_list % per_device
    )
    pool_index = jnp.where(in_use, pool_index, -1).astype(jnp.int32)
    row_total = prim_pos.shape[1]
    norm_scale = 1.0 / math.sqrt(LIST * BS)
    prim = jnp.concatenate([prim_pos, (prim_weight * norm_scale)[None, :]], axis=0).T

    coefficients = pair_sums(pool_index, pool_counts, block_pool, prim)
    feat_width = coefficients.shape[1]
    capacity = max(2, 2 * row_total // (box_count * help_count))
    regions = region_of[:, 0]
    row_order = jnp.arange(row_total, dtype=jnp.int32)
    earlier = row_order[:, None] > row_order[None, :]
    same_region = regions[:, None] == regions[None, :]
    row_rank = jnp.sum((earlier & same_region).astype(jnp.int32), axis=1)
    row_slots = regions * capacity + row_rank
    outgoing = (
        jnp.zeros((box_count * help_count * capacity, feat_width), jnp.bfloat16)
        .at[row_slots]
        .set(coefficients)
    )
    outgoing = outgoing.reshape(box_count, help_count, capacity, feat_width)
    incoming = lax.all_to_all(
        lax.all_to_all(outgoing, "box", split_axis=0, concat_axis=0, tiled=True),
        "help",
        split_axis=1,
        concat_axis=1,
        tiled=True,
    )
    owner_rows = incoming.reshape(-1, feat_width)
    region_sum = gram_by_order(owner_rows)
    region_tensor = (region_sum * (1.0 / PRIM_DEV)).reshape(1, -1)
    return (coefficients, region_tensor)


def solution(mesh):
    placed = (
        P(None, ("box", "help")),
        P(("box", "help")),
        P(("box", "help"), None, None),
        P(("box", "help"), None),
        P(("box", "help")),
        P(("box", "help"), None),
        P(("box", "help"), None),
    )
    return jax.shard_map(
        shards,
        mesh=mesh,
        in_specs=placed,
        out_specs=(P(("box", "help"), None), P(("box", "help"), None)),
        check_vma=False,
    )
```

profile of v0, /device:TPU:1, one launch (start us, length us, event | category | flops | bytes accessed | tf_op | source)
XLA Modules:
  0.0 144.8 jit_solution(4633643378818666769)
XLA Ops:
  0.6 0.7 convert_element_type.12
  1.3 0.8 fusion.36
  2.0 0.7 copy.19
  2.8 0.1 broadcast_in_dim.12
  2.9 4.7 %all_gather.3 = f32[16,8,128]{2,1,0:T(8,128)S(1)} all-gather(f32[8,8,128]{2,1,0:T(8,128)S(1)} %pad_maximum_fusion), channel_id=1, replica_groups=mesh['box'=128,'help'=2] {'help'}, dimensions={0}, use_global_device_ids=true | all-gather | bytes 98304 | tf_op jit(solution)/shard_map/all_gather | solution.py:264
  7.6 8.5 %collective-permute-start.1 = (f32[16,8,128]{2,1,0:T(8,128)S(1)}, f32[16,8,128]{2,1,0:T(8,128)S(1)}, u32[]{:S(2)}, u32[]{:S(2)}) collective-permute-start(f32[16,8,128]{2,1,0:T(8,128)S(1)} %all_gather.3), channel_id=1, source_target_pairs={{2,0},{4,2},{6,4},{8,6},{10,8},{12,10},{14,12},{16,14},{18,16},{20... | collective-permute-start | bytes 196616 | tf_op jit(solution)/shard_map/ppermute | solution.py:33
  16.1 0.0 collective-permute-start
  16.1 0.7 multiply_bitcast_fusion
  16.7 0.9 convert_reduce_fusion
  17.7 0.7 fusion.46
  18.3 0.7 compare_select_fusion.1.pick_ref
  19.0 0.7 pad_maximum_fusion.1
  19.7 0.1 copy.20
  19.8 4.8 %collective-permute-done = f32[16,8,128]{2,1,0:T(8,128)S(1)} collective-permute-done((f32[16,8,128]{2,1,0:T(8,128)S(1)}, f32[16,8,128]{2,1,0:T(8,128)S(1)}, u32[]{:S(2)}, u32[]{:S(2)}) %collective-permute-start) | collective-permute-done | bytes 65568 | tf_op jit(solution)/shard_map/ppermute | solution.py:31
  24.6 0.0 collective-permute-done.1
  24.7 0.9 fusion.35.count_ref
  25.6 14.8 %pair_sums.1 = bf16[64,1936]{1,0:T(8,128)(2,1)} custom-call(s32[4,12]{1,0:T(4,128)S(1)} %compare_select_fusion.1.pick_ref, s32[48]{0:T(128)S(1)} %fusion.35.count_ref, f32[48,8,128]{2,1,0:T(8,128)S(1)} %constant_dynamic-update-slice_fusion.pool_ref, f32[64,4]{1,0:T(8,128)S(1)} %bitcast.13), custom_call_target="tpu_custom_call" | custom-call | tf_op jit(solution)/shard_map/pair_sums/pallas_call | solution.py:209
  40.4 2.2 %scatter_custom_fusion = bf16[512,1936]{1,0:T(8,128)(2,1)S(1)} fusion(s32[64]{0:T(128)S(1)} %fusion.46, bf16[64,1936]{1,0:T(8,128)(2,1)} %pair_sums.1, bf16[]{:T(256)} %constant.79.clone.1), kind=kCustom, calls=%fused_computation.11 | custom fusion | bytes 1982976 | tf_op jit(solution)/shard_map/scatter | solution.py:293
  42.6 2.7 %reshape.184 = bf16[128,2,2,1936]{3,2,1,0:T(2,128)(2,1)} reshape(bf16[512,1936]{1,0:T(8,128)(2,1)S(1)} %scatter_custom_fusion) | data formatting | bytes 3964928 | tf_op jit(solution)/shard_map/reshape | solution.py:295
  45.3 55.7 %all_to_all.10 = bf16[128,2,2,1936]{3,2,1,0:T(2,128)(2,1)S(1)} all-to-all(bf16[128,2,2,1936]{3,2,1,0:T(2,128)(2,1)} %reshape.184), channel_id=1, replica_groups=mesh['box'=128,'help'=2] {'box'}, dimensions={0} | all-to-all | bytes 3964928 | tf_op jit(solution)/shard_map/all_to_all | solution.py:297
  101.0 4.0 %copy.21 = bf16[128,2,2,1936]{0,3,2,1:T(8,128)(2,1)} copy(bf16[128,2,2,1936]{3,2,1,0:T(2,128)(2,1)S(1)} %all_to_all.10) | data formatting | bytes 3964928 | tf_op jit(solution)/shard_map/all_to_all | solution.py:297
  105.0 12.5 %all_to_all.11 = bf16[128,2,2,1936]{0,3,2,1:T(8,128)(2,1)} all-to-all(bf16[128,2,2,1936]{0,3,2,1:T(8,128)(2,1)} %copy.21), channel_id=1, replica_groups=mesh['box'=128,'help'=2] {'help'}, dimensions={1} | all-to-all | bytes 3964928 | tf_op jit(solution)/shard_map/all_to_all | solution.py:296
  117.5 5.0 %copy.22 = bf16[128,2,2,1936]{3,2,1,0:T(2,128)(2,1)S(1)} copy(bf16[128,2,2,1936]{0,3,2,1:T(8,128)(2,1)} %all_to_all.11) | data formatting | bytes 3964928 | tf_op jit(solution)/shard_map/all_to_all | solution.py:296
  122.6 2.7 %reshape.185 = bf16[512,1936]{1,0:T(8,128)(2,1)} reshape(bf16[128,2,2,1936]{3,2,1,0:T(2,128)(2,1)S(1)} %copy.22) | data formatting | bytes 3964928 | tf_op jit(solution)/shard_map/reshape | solution.py:303
  125.3 0.0 copy-start
  125.3 1.4 fusion.11
  126.7 1.3 fusion.14
  127.9 1.3 fusion.17
  129.2 1.4 fusion.20
  130.6 1.3 fusion.23
  131.9 1.4 fusion.26
  133.3 1.3 fusion.29
  134.6 1.3 fusion.32
  135.9 1.5 %fusion.3 = f32[144,144]{1,0:T(8,128)S(1)} fusion(bf16[512,1936]{1,0:T(8,128)(2,1)} %reshape.185), kind=kOutput, calls=%fused_computation.14 | convolution fusion | flops 21233664 | bytes 345088 | tf_op jit(solution)/shard_map/dot_general | solution.py:235
  137.5 1.6 %fusion.6 = f32[160,160]{1,0:T(8,128)S(1)} fusion(bf16[512,1936]{1,0:T(8,128)(2,1)} %reshape.185), kind=kOutput, calls=%fused_computation.17 | convolution fusion | flops 26214400 | bytes 364544 | tf_op jit(solution)/shard_map/dot_general | solution.py:235
  139.0 0.0 copy-done
  139.1 0.2 fusion.8
  139.3 0.2 convolution_add_fusion.9
  139.5 0.1 concatenate.54
  139.6 0.3 convolution_add_fusion.8
  139.9 0.1 concatenate.53
  139.9 0.2 convolution_add_fusion.7
  140.2 0.1 concatenate.52
  140.3 0.3 convolution_add_fusion.6
  140.6 0.1 concatenate.51
  140.6 0.2 convolution_add_fusion.5
  140.9 0.1 concatenate.50
  141.0 0.3 convolution_add_fusion.4
  141.3 0.1 concatenate.49
  141.4 0.2 convolution_add_fusion.3
  141.6 0.1 concatenate.48
  141.8 0.3 convolution_add_fusion.2
  142.1 0.2 convolution_add_fusion.1
  142.3 0.2 concatenate.46
  142.5 0.4 convolution_add_fusion
  142.9 0.2 concatenate.45
  143.1 0.2 concatenate.44
  143.6 1.2 broadcast_multiply_fusion
  (15 shorter events, 0.2 us)
Async XLA Ops:
  7.6 17.1 %collective-permute-start.1 = (f32[16,8,128]{2,1,0:T(8,128)S(1)}, f32[16,8,128]{2,1,0:T(8,128)S(1)}, u32[]{:S(2)}, u32[]{:S(2)}) collective-permute-start(f32[16,8,128]{2,1,0:T(8,128)S(1)} %all_gather.3), channel_id=1, source_target_pairs={{2,0},{4,2},{6,4},{8,6},{10,8},{12,10},{14,12},{16,14},{18,16},{20... | collective-permute-start | bytes 196616 | tf_op jit(solution)/shard_map/ppermute | solution.py:33
  16.1 8.5 %collective-permute-start = (f32[16,8,128]{2,1,0:T(8,128)S(1)}, f32[16,8,128]{2,1,0:T(8,128)S(1)}, u32[]{:S(2)}, u32[]{:S(2)}) collective-permute-start(f32[16,8,128]{2,1,0:T(8,128)S(1)} %all_gather.3), channel_id=1, source_target_pairs={{0,2},{2,4},{4,6},{6,8},{8,10},{10,12},{12,14},{14,16},{16,18},{18... | collective-permute-start | bytes 196616 | tf_op jit(solution)/shard_map/ppermute | solution.py:31
  125.3 13.7 %copy-start = (bf16[512,1936]{1,0:T(8,128)(2,1)S(1)}, bf16[512,1936]{1,0:T(8,128)(2,1)}, u32[]{:S(2)}) copy-start(bf16[512,1936]{1,0:T(8,128)(2,1)} %reshape.185) | copy-start | bytes 5947396
where the time goes:
time: 146 us; the launch traced here: 145 us
  blocking collectives  73 us (50%)
  local copies, waits for them, and re-layouts  19 us (13%)
  matrix products  16.6 us (11%)
  Pallas kernels  14.8 us (10%)
  starting transfers between devices  8.49 us (6%)
  other arithmetic  7.24 us (5%)
  waiting for transfers between devices  4.81 us (3%)
    all_to_all x1, blocking collectives, shards(): lax.all_to_all(outgoing, 'box', split_axis=0, concat_axis=0, tiled=True)  55.7 us
    dot_general x21, matrix products, self_product(): lax.dot_general(left_rows, right_rows, (((0,), (0,)), ((), ())), preferre...  16.6 us
    pallas_call x1, Pallas kernels, pair_sums(): pl.pallas_call(pair_kernel, out_shape=jax.ShapeDtypeStruct((tiles * PT, F...  14.8 us
    all_to_all x1, blocking collectives, shards(): lax.all_to_all(lax.all_to_all(outgoing, 'box', split_axis=0, concat_axis=...  12.5 us
    ppermute x1, starting transfers between devices, padded(): lax.ppermute(head, axis, [((i + 1) % count, i) for i in range(count)])  8.49 us
    all_to_all x1, local copies, waits for them, and re-layouts, shards(): lax.all_to_all(lax.all_to_all(outgoing, 'box', split_axis=0, concat_axis=...  5.02 us
    ppermute x1, waiting for transfers between devices, padded(): lax.ppermute(tail, axis, [(i, (i + 1) % count) for i in range(count)])  4.8 us
    all_gather x1, blocking collectives, shards(): chip_pool = lax.all_gather(own_blocks, 'help', axis=0, tiled=True)  4.75 us
  transfers between devices with their start and end apart: 2, of which 1 were waited for; matrix products, arithmetic and copies ran while one was open for 3% of the time, Pallas kernels for 0%

commit v1 on v0

--- a/solution.py
+++ b/solution.py
@@ -231,22 +231,94 @@
     )(pick, counts, pool, prim)
 
 
-def self_product(left_rows, right_rows):
-    return lax.dot_general(
-        left_rows, right_rows, (((0,), (0,)), ((), ())), preferred_element_type=jnp.float32
-    )
-
-
-def gram_by_order(owner_rows):
-    pieces = []
+def gram_kernel(rows_ref, out_ref, feats, gram):
+    row_total = rows_ref.shape[0]
+    row = lax.broadcasted_iota(jnp.int32, (256, 256), 0)
+    col = lax.broadcasted_iota(jnp.int32, (256, 256), 1)
+    turn = jnp.where(col == (row % 16) * 16 + row // 16, 1.0, 0.0).astype(jnp.bfloat16)
+
+    def regroup(step, carry):
+        at = pl.multiple_of(step * 16, 16)
+        block = rows_ref[pl.ds(at, 16)].reshape(256, 128)
+        moved = jnp.dot(turn, block, preferred_element_type=jnp.float32).astype(jnp.bfloat16)
+        feats[:, pl.ds(at, 16), :] = moved.reshape(16, 16, 128)
+        return carry
+
+    lax.fori_loop(0, row_total // 16, regroup, 0)
+    row = lax.broadcasted_iota(jnp.int32, (128, 128), 0)
+    col = lax.broadcasted_iota(jnp.int32, (128, 128), 1)
+
+    def one_hot(cond):
+        return jnp.where(cond, 1.0, 0.0).astype(jnp.bfloat16)
+
+    def aligned(start, width):
+        group, skip = start // 128, start % 128
+        here, there = one_hot(row == col + skip), one_hot(row + 128 == col + skip)
+        here_t, there_t = one_hot(col == row + skip), one_hot(col + 128 == row + skip)
+        across = (((1,), (1,)), ((), ()))
+        plain = jnp.dot(feats[group], here, preferred_element_type=jnp.float32)
+        flipped = lax.dot_general(here_t, feats[group], across, preferred_element_type=jnp.float32)
+        if skip + width > 128:
+            plain += jnp.dot(feats[group + 1], there, preferred_element_type=jnp.float32)
+            flipped += lax.dot_general(
+                there_t, feats[group + 1], across, preferred_element_type=jnp.float32
+            )
+        return plain.astype(jnp.bfloat16), flipped.astype(jnp.bfloat16)
+
+    base = 0
     for cos_start, sin_start, length in order_slices(LMAX, NBIN):
-        cos_rows = owner_rows[:, cos_start : cos_start + length]
-        gram_block = self_product(cos_rows, cos_rows)
-        if sin_start >= 0:
-            sine_rows = owner_rows[:, sin_start : sin_start + length]
-            gram_block = gram_block + self_product(sine_rows, sine_rows)
-        pieces.append(gram_block.reshape(-1))
-    return jnp.concatenate(pieces)
+        count = length // NBIN
+        parts = -(-length // 128)
+        for kind_start in (cos_start, sin_start):
+            if kind_start < 0:
+                continue
+            tiles = [
+                aligned(kind_start + 128 * part, min(128, length - 128 * part))
+                for part in range(parts)
+            ]
+            for up in range(parts):
+                for over in range(parts):
+                    product = jnp.dot(
+                        tiles[up][1], tiles[over][0], preferred_element_type=jnp.float32
+                    )
+                    at = (over, slice(up * 128, up * 128 + 128))
+                    if kind_start == cos_start:
+                        gram[at] = product
+                    else:
+                        gram[at] += product
+        lane = lax.broadcasted_iota(jnp.int32, (2 * count, 128), 1)
+        for rest in range(8):
+            for part in range(parts):
+                units = min(8, count - 8 * part)
+                shift = rest * count % 8
+                at = base + rest * count // 8 + part
+                value = gram[part, pl.ds(rest, 2 * count, stride=8), :] * (1.0 / PRIM_DEV)
+                if shift:
+                    value = pltpu.roll(value, 16 * shift, 1)
+                window = pl.ds(at, 2 * count, stride=count)
+                keep = (lane >= 16 * shift) & (lane < 16 * (shift + units))
+                out_ref[window, :] = jnp.where(keep, value, out_ref[window, :])
+                if shift + units > 8:
+                    window = pl.ds(at + 1, 2 * count, stride=count)
+                    keep = lane < 16 * (shift + units - 8)
+                    out_ref[window, :] = jnp.where(keep, value, out_ref[window, :])
+        base += 2 * count * count
+
+
+def gram_rows(rows):
+    total = sum(length * length for _, _, length in order_slices(LMAX, NBIN))
+    return pl.pallas_call(
+        gram_kernel,
+        out_shape=jax.ShapeDtypeStruct((total // 128, 128), jnp.float32),
+        in_specs=[pl.BlockSpec(memory_space=pltpu.VMEM)],
+        out_specs=pl.BlockSpec(memory_space=pltpu.VMEM),
+        scratch_shapes=[
+            pltpu.VMEM((16, rows.shape[0], 128), jnp.bfloat16),
+            pltpu.VMEM((2, 256, 128), jnp.float32),
+        ],
+        compiler_params=pltpu.CompilerParams(vmem_limit_bytes=40 << 20),
+        name="gram_rows",
+    )(rows)
 
 
 def shards(prim_pos, prim_weight, sec_pos, sec_weight, sec_counts, tile_lists, region_of):
@@ -301,8 +373,8 @@
         tiled=True,
     )
     owner_rows = incoming.reshape(-1, feat_width)
-    region_sum = gram_by_order(owner_rows)
-    region_tensor = (region_sum * (1.0 / PRIM_DEV)).reshape(1, -1)
+    owner_rows = jnp.pad(owner_rows, ((0, 0), (0, WIDE - feat_width))).reshape(-1, 16, 128)
+    region_tensor = gram_rows(owner_rows).reshape(1, -1)
     return (coefficients, region_tensor)
 
 

time: 146 us -> 140 us (0.959)
  matrix products: 16.6 us -> 0 us
  Pallas kernels: 14.8 us -> 24.8 us
  local copies, waits for them, and re-layouts: 19 us -> 21.2 us
    dot_general x21 -> x0, matrix products: 16.6 us -> none  [self_product(): lax.dot_general(left_rows, right_rows, (((0,), (0,)), ((), ())), preferre...]
    pallas_call x0 -> x1, Pallas kernels: none -> 11.4 us  [gram_rows(): pl.pallas_call(gram_kernel, out_shape=jax.ShapeDtypeStruct((total // 128,...]
    unnamed x15 -> x6, local copies, waits for them, and re-layouts: 0.84 us -> 4.42 us
where the time goes in v1:
time: 140 us; the launch traced here: 139 us
  blocking collectives  72.9 us (52%)
  Pallas kernels  24.8 us (18%)
  local copies, waits for them, and re-layouts  21.2 us (15%)
  starting transfers between devices  8.49 us (6%)
  other arithmetic  6.01 us (4%)
  waiting for transfers between devices  4.81 us (3%)
    all_to_all x1, blocking collectives, shards(): lax.all_to_all(outgoing, 'box', split_axis=0, concat_axis=0, tiled=True)  55 us
    pallas_call x1, Pallas kernels, pair_sums(): pl.pallas_call(pair_kernel, out_shape=jax.ShapeDtypeStruct((tiles * PT, F...  13.4 us
    all_to_all x1, blocking collectives, shards(): lax.all_to_all(lax.all_to_all(outgoing, 'box', split_axis=0, concat_axis=...  13.2 us
    pallas_call x1, Pallas kernels, gram_rows(): pl.pallas_call(gram_kernel, out_shape=jax.ShapeDtypeStruct((total // 128,...  11.4 us
    ppermute x1, starting transfers between devices, padded(): lax.ppermute(head, axis, [((i + 1) % count, i) for i in range(count)])  8.49 us
    all_to_all x1, local copies, waits for them, and re-layouts, shards(): lax.all_to_all(lax.all_to_all(outgoing, 'box', split_axis=0, concat_axis=...  5.02 us
    ppermute x1, waiting for transfers between devices, padded(): lax.ppermute(tail, axis, [(i, (i + 1) % count) for i in range(count)])  4.8 us
    all_gather x1, blocking collectives, shards(): chip_pool = lax.all_gather(own_blocks, 'help', axis=0, tiled=True)  4.75 us
  transfers between devices with their start and end apart: 2, of which 1 were waited for; matrix products, arithmetic and copies ran while one was open for 3% of the time, Pallas kernels for 0%

profile of v1, /device:TPU:1, one launch (start us, length us, event | category | flops | bytes accessed | tf_op | source)
XLA Modules:
  0.0 138.9 jit_solution(7394742658765042861)
XLA Ops:
  0.6 0.7 convert_element_type.14
  1.3 0.8 fusion.4
  2.0 0.7 copy.19
  2.8 0.1 broadcast_in_dim.12
  2.9 4.7 %all_gather.3 = f32[16,8,128]{2,1,0:T(8,128)S(1)} all-gather(f32[8,8,128]{2,1,0:T(8,128)S(1)} %pad_maximum_fusion), channel_id=1, replica_groups=mesh['box'=128,'help'=2] {'help'}, dimensions={0}, use_global_device_ids=true | all-gather | bytes 98304 | tf_op jit(solution)/shard_map/all_gather | solution.py:336
  7.6 8.5 %collective-permute-start.1 = (f32[16,8,128]{2,1,0:T(8,128)S(1)}, f32[16,8,128]{2,1,0:T(8,128)S(1)}, u32[]{:S(2)}, u32[]{:S(2)}) collective-permute-start(f32[16,8,128]{2,1,0:T(8,128)S(1)} %all_gather.3), channel_id=1, source_target_pairs={{2,0},{4,2},{6,4},{8,6},{10,8},{12,10},{14,12},{16,14},{18,16},{20... | collective-permute-start | bytes 196616 | tf_op jit(solution)/shard_map/ppermute | solution.py:33
  16.1 0.0 collective-permute-start
  16.1 0.7 multiply_bitcast_fusion
  16.7 0.9 convert_reduce_fusion
  17.7 0.7 fusion.14
  18.3 0.7 compare_select_fusion.1.pick_ref
  19.0 0.7 pad_maximum_fusion.1
  19.7 0.1 copy.20
  19.8 4.8 %collective-permute-done = f32[16,8,128]{2,1,0:T(8,128)S(1)} collective-permute-done((f32[16,8,128]{2,1,0:T(8,128)S(1)}, f32[16,8,128]{2,1,0:T(8,128)S(1)}, u32[]{:S(2)}, u32[]{:S(2)}) %collective-permute-start) | collective-permute-done | bytes 65568 | tf_op jit(solution)/shard_map/ppermute | solution.py:31
  24.6 0.0 collective-permute-done.1
  24.7 0.9 fusion.3.count_ref
  25.6 13.4 %pair_sums.1 = bf16[64,1936]{1,0:T(8,128)(2,1)} custom-call(s32[4,12]{1,0:T(4,128)S(1)} %compare_select_fusion.1.pick_ref, s32[48]{0:T(128)S(1)} %fusion.3.count_ref, f32[48,8,128]{2,1,0:T(8,128)S(1)} %constant_dynamic-update-slice_fusion.pool_ref, f32[64,4]{1,0:T(8,128)S(1)} %bitcast.22), custom_call_target="tpu_custom_call" | custom-call | tf_op jit(solution)/shard_map/pair_sums/pallas_call | solution.py:209
  39.1 2.2 %scatter_custom_fusion = bf16[512,1936]{1,0:T(8,128)(2,1)S(1)} fusion(s32[64]{0:T(128)S(1)} %fusion.14, bf16[64,1936]{1,0:T(8,128)(2,1)} %pair_sums.1, bf16[]{:T(256)} %constant.79.clone.1), kind=kCustom, calls=%fused_computation.2 | custom fusion | bytes 1982976 | tf_op jit(solution)/shard_map/scatter | solution.py:365
  41.3 2.7 %reshape.21 = bf16[128,2,2,1936]{3,2,1,0:T(2,128)(2,1)} reshape(bf16[512,1936]{1,0:T(8,128)(2,1)S(1)} %scatter_custom_fusion) | data formatting | bytes 3964928 | tf_op jit(solution)/shard_map/reshape | solution.py:367
  43.9 55.0 %all_to_all.10 = bf16[128,2,2,1936]{3,2,1,0:T(2,128)(2,1)S(1)} all-to-all(bf16[128,2,2,1936]{3,2,1,0:T(2,128)(2,1)} %reshape.21), channel_id=1, replica_groups=mesh['box'=128,'help'=2] {'box'}, dimensions={0} | all-to-all | bytes 3964928 | tf_op jit(solution)/shard_map/all_to_all | solution.py:369
  98.9 4.0 %copy.21 = bf16[128,2,2,1936]{0,3,2,1:T(8,128)(2,1)} copy(bf16[128,2,2,1936]{3,2,1,0:T(2,128)(2,1)S(1)} %all_to_all.10) | data formatting | bytes 3964928 | tf_op jit(solution)/shard_map/all_to_all | solution.py:369
  102.9 13.2 %all_to_all.11 = bf16[128,2,2,1936]{0,3,2,1:T(8,128)(2,1)} all-to-all(bf16[128,2,2,1936]{0,3,2,1:T(8,128)(2,1)} %copy.21), channel_id=1, replica_groups=mesh['box'=128,'help'=2] {'help'}, dimensions={1} | all-to-all | bytes 3964928 | tf_op jit(solution)/shard_map/all_to_all | solution.py:368
  116.1 5.0 %copy.22 = bf16[128,2,2,1936]{3,2,1,0:T(2,128)(2,1)S(1)} copy(bf16[128,2,2,1936]{0,3,2,1:T(8,128)(2,1)} %all_to_all.11) | data formatting | bytes 3964928 | tf_op jit(solution)/shard_map/all_to_all | solution.py:368
  121.1 2.7 %reshape.22 = bf16[512,1936]{1,0:T(8,128)(2,1)} reshape(bf16[128,2,2,1936]{3,2,1,0:T(2,128)(2,1)S(1)} %copy.22) | data formatting | bytes 3964928 | tf_op jit(solution)/shard_map/reshape | solution.py:375
  123.9 1.8 %pad_bitcast_fusion = bf16[64,8,16,128]{3,1,2,0:T(8,128)(2,1)S(1)} fusion(bf16[512,1936]{1,0:T(8,128)(2,1)} %reshape.22), kind=kLoop, calls=%fused_computation.1 | loop fusion | bytes 4079616
  125.6 0.6 copy.23
  126.2 11.4 %gram_rows.1 = f32[1012,128]{1,0:T(8,128)S(1)} custom-call(bf16[512,16,128]{2,1,0:T(8,128)(2,1)S(1)} %bitcast.20), custom_call_target="tpu_custom_call" | custom-call | tf_op jit(solution)/shard_map/gram_rows/pallas_call | solution.py:310
  137.6 1.3 copy.26
  (4 shorter events, 0.0 us)
Async XLA Ops:
  7.6 17.1 %collective-permute-start.1 = (f32[16,8,128]{2,1,0:T(8,128)S(1)}, f32[16,8,128]{2,1,0:T(8,128)S(1)}, u32[]{:S(2)}, u32[]{:S(2)}) collective-permute-start(f32[16,8,128]{2,1,0:T(8,128)S(1)} %all_gather.3), channel_id=1, source_target_pairs={{2,0},{4,2},{6,4},{8,6},{10,8},{12,10},{14,12},{16,14},{18,16},{20... | collective-permute-start | bytes 196616 | tf_op jit(solution)/shard_map/ppermute | solution.py:33
  16.1 8.5 %collective-permute-start = (f32[16,8,128]{2,1,0:T(8,128)S(1)}, f32[16,8,128]{2,1,0:T(8,128)S(1)}, u32[]{:S(2)}, u32[]{:S(2)}) collective-permute-start(f32[16,8,128]{2,1,0:T(8,128)S(1)} %all_gather.3), channel_id=1, source_target_pairs={{0,2},{2,4},{4,6},{6,8},{8,10},{10,12},{12,14},{14,16},{16,18},{18... | collective-permute-start | bytes 196616 | tf_op jit(solution)/shard_map/ppermute | solution.py:31

commit v2 on v1

--- a/solution.py
+++ b/solution.py
@@ -72,7 +72,15 @@
     return order_slices(LMAX, 1)[m_order][0]
 
 
-def pair_kernel(pick_ref, count_ref, pool_ref, prim_ref, coef_ref, packed, basis, spline, acc, diag, spread):
+def turn_matrix():
+    row = lax.broadcasted_iota(jnp.int32, (256, 256), 0)
+    col = lax.broadcasted_iota(jnp.int32, (256, 256), 1)
+    return jnp.where(col == (row % 16) * 16 + row // 16, 1.0, 0.0).astype(jnp.bfloat16)
+
+
+def pair_kernel(
+    pick_ref, count_ref, pool_ref, prim_ref, coef_ref, rows_ref, packed, basis, spline, acc, diag, spread
+):
     tile = pl.program_id(0)
     lane = lax.broadcasted_iota(jnp.int32, (8, BS), 1)
 
@@ -202,13 +210,18 @@
     for group in range(15):
         coef_ref[:, group * 128 : (group + 1) * 128] = rows[group * PT : (group + 1) * PT, :]
     coef_ref[:, 1920:FEAT] = rows[15 * PT : 16 * PT, : FEAT - 1920]
+    turned = jnp.dot(turn_matrix(), rows, preferred_element_type=jnp.float32)
+    rows_ref[...] = turned.astype(jnp.bfloat16).reshape(PT, 16, 128)
 
 
 def pair_sums(pick, counts, pool, prim):
     tiles = pick.shape[0]
     return pl.pallas_call(
         pair_kernel,
-        out_shape=jax.ShapeDtypeStruct((tiles * PT, FEAT), jnp.bfloat16),
+        out_shape=(
+            jax.ShapeDtypeStruct((tiles * PT, FEAT), jnp.bfloat16),
+            jax.ShapeDtypeStruct((tiles * PT, 16, 128), jnp.bfloat16),
+        ),
         grid_spec=pltpu.PrefetchScalarGridSpec(
             num_scalar_prefetch=2,
             grid=(tiles,),
@@ -216,7 +229,10 @@
                 pl.BlockSpec(pool.shape, lambda t, *_: (0, 0, 0)),
                 pl.BlockSpec((PT, prim.shape[1]), lambda t, *_: (t, 0)),
             ],
-            out_specs=pl.BlockSpec((PT, FEAT), lambda t, *_: (t, 0)),
+            out_specs=(
+                pl.BlockSpec((PT, FEAT), lambda t, *_: (t, 0)),
+                pl.BlockSpec((PT, 16, 128), lambda t, *_: (t, 0, 0)),
+            ),
             scratch_shapes=[
                 pltpu.VMEM((2 * ((LIST + 1) // 2) + 2, 8, BS), jnp.float32),
                 pltpu.VMEM((NHARM * PT, 2 * BS), jnp.bfloat16),
@@ -231,11 +247,149 @@
     )(pick, counts, pool, prim)
 
 
+Z_SIZE = 8
+PLANE = 16
+SOURCE_MOVES = (0, -1, 1, -2, 2, -3, 3, 4)
+PEERS = 2 * PLANE
+MESH = pl.DeviceIdType.MESH
+
+
+def exchange_kernel(table_ref, rows_ref, out_ref, *scratch):
+    held = (rows_ref,) + scratch[:7]
+    stage, ring_send, ring_recv, plane_send, plane_recv = scratch[7:]
+    box, core = lax.axis_index("box"), lax.axis_index("help")
+    z_at, x_at, y_at = box // PLANE, (box // 4) % 4, box % 4
+    ring = (
+        ((z_at + 1) % Z_SIZE * PLANE + box % PLANE, core),
+        ((z_at + Z_SIZE - 1) % Z_SIZE * PLANE + box % PLANE, core),
+    )
+
+    def peer(turn):
+        x_to, y_to = (x_at + turn // 8) % 4, (y_at + turn // 2 % 4) % 4
+        return (z_at * PLANE + x_to * 4 + y_to, (core + turn % 2) % 2)
+
+    barrier = pltpu.get_barrier_semaphore()
+    for way in range(2):
+        pl.semaphore_signal(barrier, inc=1, device_id=ring[way], device_id_type=MESH)
+
+    def greet(turn, carry):
+        pl.semaphore_signal(barrier, inc=1, device_id=peer(turn), device_id_type=MESH)
+        return carry
+
+    lax.fori_loop(1, PEERS, greet, 0)
+    pl.semaphore_wait(barrier, PEERS + 1)
+
+    def ring_copy(way, step, half):
+        from_at = 0 if step == 1 else 2 * (step - 1) - 1 + way
+        to_at = 7 if step == 4 else 2 * step - 1 + way
+        part = pl.ds(half * (PRIM_DEV // 2), PRIM_DEV // 2)
+        return pltpu.make_async_remote_copy(
+            src_ref=held[from_at].at[part],
+            dst_ref=held[to_at].at[part],
+            send_sem=ring_send.at[way, step - 1, half],
+            recv_sem=ring_recv.at[way, step - 1, half],
+            device_id=ring[way],
+            device_id_type=MESH,
+        )
+
+    def deal(batch, first, number):
+        def fill(turn, target):
+            for source in range(first, first + number):
+                z_from = (z_at + SOURCE_MOVES[source] + Z_SIZE) % Z_SIZE
+                for slot in range(2):
+                    row = table_ref[z_from * (2 * PEERS) + turn * 2 + slot]
+                    value = held[source][jnp.maximum(row, 0)]
+                    target[turn, source, slot] = jnp.where(row >= 0, value, jnp.zeros_like(value))
+
+        fill(0, out_ref)
+
+        def one_peer(count, carry):
+            turn = count * 13 % PEERS
+            fill(turn, stage)
+            pltpu.make_async_remote_copy(
+                src_ref=stage.at[turn, pl.ds(first, number)],
+                dst_ref=out_ref.at[turn, pl.ds(first, number)],
+                send_sem=plane_send.at[batch],
+                recv_sem=plane_recv.at[batch],
+                device_id=peer(turn),
+                device_id_type=MESH,
+            ).start()
+            return carry
+
+        lax.fori_loop(1, PEERS, one_peer, 0)
+
+    for half in range(2):
+        for way in range(2):
+            ring_copy(way, 1, half).start()
+    deal(0, 0, 1)
+    for step in range(1, 4):
+        for half in range(2):
+            for way in range(2):
+                ring_copy(way, step, half).wait_recv()
+                if step < 3 or half == way:
+                    ring_copy(way, step + 1, half).start()
+        deal(step, 2 * step - 1, 2)
+    for way in range(2):
+        ring_copy(way, 4, way).wait_recv()
+    deal(4, 7, 1)
+    for step in range(1, 5):
+        for half in range(2):
+            for way in range(2):
+                if step < 4 or half == way:
+                    ring_copy(way, step, half).wait_send()
+    for batch, first, number in ((0, 0, 1), (1, 1, 2), (2, 3, 2), (3, 5, 2), (4, 7, 1)):
+        sent = stage.at[pl.ds(1, PEERS - 1), pl.ds(first, number)]
+        pltpu.make_async_copy(sent, sent, plane_send.at[batch]).wait()
+        come = out_ref.at[pl.ds(1, PEERS - 1), pl.ds(first, number)]
+        pltpu.make_async_copy(come, come, plane_recv.at[batch]).wait()
+
+
+def exchange(table, rows):
+    shape = (PEERS, Z_SIZE, 2, 16, 128)
+    return pl.pallas_call(
+        exchange_kernel,
+        out_shape=jax.ShapeDtypeStruct(shape, rows.dtype),
+        in_specs=[
+            pl.BlockSpec(memory_space=pltpu.SMEM),
+            pl.BlockSpec(memory_space=pltpu.VMEM),
+        ],
+        out_specs=pl.BlockSpec(memory_space=pltpu.VMEM),
+        scratch_shapes=[pltpu.VMEM(rows.shape, rows.dtype)] * 7
+        + [
+            pltpu.VMEM(shape, rows.dtype),
+            pltpu.SemaphoreType.DMA((2, 4, 2)),
+            pltpu.SemaphoreType.DMA((2, 4, 2)),
+            pltpu.SemaphoreType.DMA((5,)),
+            pltpu.SemaphoreType.DMA((5,)),
+        ],
+        compiler_params=pltpu.CompilerParams(
+            collective_id=1, has_side_effects=True, vmem_limit_bytes=40 << 20
+        ),
+        name="exchange",
+    )(table, rows)
+
+
+def row_table(regions):
+    box, core = lax.axis_index("box"), lax.axis_index("help")
+    row_total = regions.shape[0]
+    row_order = jnp.arange(row_total, dtype=jnp.int32)
+    earlier = row_order[:, None] > row_order[None, :]
+    same_region = regions[:, None] == regions[None, :]
+    row_rank = jnp.sum((earlier & same_region).astype(jnp.int32), axis=1)
+    code = regions * 2 + row_rank
+    lines = [[at + PLANE * z for z in range(Z_SIZE)] for at in range(PLANE)]
+    codes = lax.all_gather(code, "box", axis_index_groups=lines)
+    turn = jnp.arange(PEERS, dtype=jnp.int32)
+    x_to, y_to = (box // 4 + turn // 8) % 4, (box + turn // 2) % 4
+    owner = (box // PLANE * PLANE + x_to * 4 + y_to) * 2 + (core + turn) % 2
+    wanted = (owner[:, None] * 2 + jnp.arange(2, dtype=jnp.int32)[None, :]).reshape(-1)
+    found = codes[:, None, :] == wanted[None, :, None]
+    return jnp.max(jnp.where(found, row_order[None, None, :], -1), axis=2).reshape(-1)
+
+
 def gram_kernel(rows_ref, out_ref, feats, gram):
     row_total = rows_ref.shape[0]
-    row = lax.broadcasted_iota(jnp.int32, (256, 256), 0)
-    col = lax.broadcasted_iota(jnp.int32, (256, 256), 1)
-    turn = jnp.where(col == (row % 16) * 16 + row // 16, 1.0, 0.0).astype(jnp.bfloat16)
+    turn = turn_matrix()
 
     def regroup(step, carry):
         at = pl.multiple_of(step * 16, 16)
@@ -350,30 +504,8 @@
     norm_scale = 1.0 / math.sqrt(LIST * BS)
     prim = jnp.concatenate([prim_pos, (prim_weight * norm_scale)[None, :]], axis=0).T
 
-    coefficients = pair_sums(pool_index, pool_counts, block_pool, prim)
-    feat_width = coefficients.shape[1]
-    capacity = max(2, 2 * row_total // (box_count * help_count))
-    regions = region_of[:, 0]
-    row_order = jnp.arange(row_total, dtype=jnp.int32)
-    earlier = row_order[:, None] > row_order[None, :]
-    same_region = regions[:, None] == regions[None, :]
-    row_rank = jnp.sum((earlier & same_region).astype(jnp.int32), axis=1)
-    row_slots = regions * capacity + row_rank
-    outgoing = (
-        jnp.zeros((box_count * help_count * capacity, feat_width), jnp.bfloat16)
-        .at[row_slots]
-        .set(coefficients)
-    )
-    outgoing = outgoing.reshape(box_count, help_count, capacity, feat_width)
-    incoming = lax.all_to_all(
-        lax.all_to_all(outgoing, "box", split_axis=0, concat_axis=0, tiled=True),
-        "help",
-        split_axis=1,
-        concat_axis=1,
-        tiled=True,
-    )
-    owner_rows = incoming.reshape(-1, feat_width)
-    owner_rows = jnp.pad(owner_rows, ((0, 0), (0, WIDE - feat_width))).reshape(-1, 16, 128)
+    coefficients, rows = pair_sums(pool_index, pool_counts, block_pool, prim)
+    owner_rows = exchange(row_table(region_of[:, 0]), rows).reshape(-1, 16, 128)
     region_tensor = gram_rows(owner_rows).reshape(1, -1)
     return (coefficients, region_tensor)
 

time: 140 us -> 101 us (0.72)
  blocking collectives: 72.9 us -> 15.8 us
  Pallas kernels: 24.8 us -> 66.6 us
  local copies, waits for them, and re-layouts: 21.2 us -> 2.4 us
  waiting for transfers between devices: 4.81 us -> 0.01 us
    all_to_all x2 -> x0, blocking collectives: 68.1 us -> none  [the longest x1 55 us: shards(): lax.all_to_all(outgoing, 'box', split_axis=0, concat_axis=0, tiled=True)]
    pallas_call x1 -> x2, Pallas kernels: 13.4 us -> 55.3 us  [the longest x1 43.1 us: exchange(): pl.pallas_call(exchange_kernel, out_shape=jax.ShapeDtypeStruct(shape, row...]
    all_gather x0 -> x1, blocking collectives: none -> 11 us  [row_table(): codes = lax.all_gather(code, 'box', axis_index_groups=lines)]
    all_to_all x2 -> x0, local copies, waits for them, and re-layouts: 9.04 us -> none  [the longest x1 5.02 us: shards(): lax.all_to_all(lax.all_to_all(outgoing, 'box', split_axis=0, concat_axis=...]
    reshape x2 -> x1, local copies, waits for them, and re-layouts: 5.41 us -> 0.08 us  [row_table(): jnp.max(jnp.where(found, row_order[None, None, :], -1), axis=2).reshape(-1)]
    ppermute x1, waiting for transfers between devices: 4.8 us -> 0.01 us  [padded(): lax.ppermute(tail, axis, [(i, (i + 1) % count) for i in range(count)])]
    unnamed x6 -> x4, local copies, waits for them, and re-layouts: 4.42 us -> 2.04 us
    scatter x1 -> x0, local copies, waits for them, and re-layouts: 2.2 us -> none  [shards(): outgoing = jnp.zeros((box_count * help_count * capacity, feat_width), jnp...]
  transfers between devices with their start and end apart: 2 -> 2, of which waited for: 1 -> 0; matrix products, arithmetic and copies ran while one was open for 3% -> 4% of each run, Pallas kernels for 0% -> 0%
where the time goes in v2:
time: 101 us; the launch traced here: 100 us
  Pallas kernels  66.6 us (66%)
  blocking collectives  15.8 us (16%)
  starting transfers between devices  8.49 us (8%)
  other arithmetic  6.39 us (6%)
  local copies, waits for them, and re-layouts  2.4 us (2%)
    pallas_call x1, Pallas kernels, exchange(): pl.pallas_call(exchange_kernel, out_shape=jax.ShapeDtypeStruct(shape, row...  43.1 us
    pallas_call x1, Pallas kernels, pair_sums(): pl.pallas_call(pair_kernel, out_shape=(jax.ShapeDtypeStruct((tiles * PT,...  12.2 us
    pallas_call x1, Pallas kernels, gram_rows(): pl.pallas_call(gram_kernel, out_shape=jax.ShapeDtypeStruct((total // 128,...  11.3 us
    all_gather x1, blocking collectives, row_table(): codes = lax.all_gather(code, 'box', axis_index_groups=lines)  11 us
    ppermute x1, starting transfers between devices, padded(): lax.ppermute(head, axis, [((i + 1) % count, i) for i in range(count)])  8.49 us
    all_gather x1, blocking collectives, shards(): chip_pool = lax.all_gather(own_blocks, 'help', axis=0, tiled=True)  4.75 us
    unnamed x4, local copies, waits for them, and re-layouts  2.04 us
  transfers between devices with their start and end apart: 2, of which 0 were waited for; matrix products, arithmetic and copies ran while one was open for 4% of the time, Pallas kernels for 0%

profile of v2, /device:TPU:1, one launch (start us, length us, event | category | flops | bytes accessed | tf_op | source)
XLA Modules:
  0.0 100.4 jit_solution(668592542019980163)
XLA Ops:
  0.6 0.7 convert_element_type.12
  1.3 0.8 fusion.2
  2.0 0.7 copy.17
  2.8 0.1 broadcast_in_dim.18
  2.9 4.7 %all_gather.7 = f32[16,8,128]{2,1,0:T(8,128)S(1)} all-gather(f32[8,8,128]{2,1,0:T(8,128)S(1)} %pad_maximum_fusion), channel_id=1, replica_groups=mesh['box'=128,'help'=2] {'help'}, dimensions={0}, use_global_device_ids=true | all-gather | bytes 98304 | tf_op jit(solution)/shard_map/all_gather | solution.py:490
  7.6 8.5 %collective-permute-start.1 = (f32[16,8,128]{2,1,0:T(8,128)S(1)}, f32[16,8,128]{2,1,0:T(8,128)S(1)}, u32[]{:S(2)}, u32[]{:S(2)}) collective-permute-start(f32[16,8,128]{2,1,0:T(8,128)S(1)} %all_gather.7), channel_id=1, source_target_pairs={{2,0},{4,2},{6,4},{8,6},{10,8},{12,10},{14,12},{16,14},{18,16},{20... | collective-permute-start | bytes 196616 | tf_op jit(solution)/shard_map/ppermute | solution.py:33
  16.1 0.0 collective-permute-start
  16.1 0.7 multiply_bitcast_fusion
  16.7 0.9 convert_reduce_fusion
  17.7 0.7 fusion.23
  18.3 0.7 compare_select_fusion.6.pick_ref
  19.0 11.0 %all-gather = s32[8,1,64]{2,1,0:T(1,128)S(1)} all-gather(s32[1,1,64]{2,1,0:T(1,128)S(1)} %fusion.23), channel_id=1, replica_groups={{0,32,64,96,128,160,192,224},{2,34,66,98,130,162,194,226},{4,36,68,100,..., dimensions={0}, use_global_device_ids=true | all-gather | bytes 2304 | tf_op jit(solution)/shard_map/all_gather | solution.py:381
  30.1 0.1 iota_add_fusion
  30.1 0.1 add.171
  30.3 0.3 select_reduce_fusion
  30.5 0.1 reshape.116.table_ref
  30.6 0.7 pad_maximum_fusion.1
  31.3 0.1 copy.18
  31.4 0.0 collective-permute-done
  31.4 0.0 collective-permute-done.1
  31.5 0.9 fusion.1.count_ref
  32.4 12.2 %pair_sums.1 = (bf16[64,1936]{1,0:T(8,128)(2,1)}, bf16[64,16,128]{2,1,0:T(8,128)(2,1)S(1)}) custom-call(s32[4,12]{1,0:T(4,128)S(1)} %compare_select_fusion.6.pick_ref, s32[48]{0:T(128)S(1)} %fusion.1.count_ref, f32[48,8,128]{2,1,0:T(8,128)S(1)} %constant_dynamic-update-slice_fusion.pool_ref, f32[64,4]{1,0:T(8,128)S(1)} %bitcast.22), custom_call_target="tpu_custom_call" | custom-call | tf_op jit(solution)/shard_map/pair_sums/pallas_call | solution.py:219
  44.6 43.1 %exchange.1 = bf16[32,8,2,16,128]{4,3,2,1,0:T(8,128)(2,1)S(1)} custom-call(s32[512]{0:T(512)S(1)} %reshape.116.table_ref, bf16[64,16,128]{2,1,0:T(8,128)(2,1)S(1)} %get-tuple-element.5.rows_ref), custom_call_target="tpu_custom_call" | custom-call | tf_op jit(solution)/shard_map/exchange/pallas_call | solution.py:349
  87.7 11.3 %gram_rows.1 = f32[1012,128]{1,0:T(8,128)S(1)} custom-call(bf16[512,16,128]{2,1,0:T(8,128)(2,1)S(1)} %bitcast.20), custom_call_target="tpu_custom_call" | custom-call | tf_op jit(solution)/shard_map/gram_rows/pallas_call | solution.py:464
  99.1 1.3 %copy.21 = f32[1,1,1012,128]{3,1,2,0:T(1,128)} copy(f32[1,1,1012,128]{3,2,1,0:T(8,128)S(1)} %bitcast.21) | data formatting | bytes 1036288
  (5 shorter events, 0.1 us)
Async XLA Ops:
  7.6 23.8 %collective-permute-start.1 = (f32[16,8,128]{2,1,0:T(8,128)S(1)}, f32[16,8,128]{2,1,0:T(8,128)S(1)}, u32[]{:S(2)}, u32[]{:S(2)}) collective-permute-start(f32[16,8,128]{2,1,0:T(8,128)S(1)} %all_gather.7), channel_id=1, source_target_pairs={{2,0},{4,2},{6,4},{8,6},{10,8},{12,10},{14,12},{16,14},{18,16},{20... | collective-permute-start | bytes 196616 | tf_op jit(solution)/shard_map/ppermute | solution.py:33
  16.1 15.3 %collective-permute-start = (f32[16,8,128]{2,1,0:T(8,128)S(1)}, f32[16,8,128]{2,1,0:T(8,128)S(1)}, u32[]{:S(2)}, u32[]{:S(2)}) collective-permute-start(f32[16,8,128]{2,1,0:T(8,128)S(1)} %all_gather.7), channel_id=1, source_target_pairs={{0,2},{2,4},{4,6},{6,8},{8,10},{10,12},{12,14},{14,16},{16,18},{18... | collective-permute-start | bytes 196616 | tf_op jit(solution)/shard_map/ppermute | solution.py:31

commit v3 on v2

--- a/solution.py
+++ b/solution.py
@@ -16,25 +16,15 @@
 PRIM_DEV = 64
 NHARM = (LMAX + 1) ** 2
 FEAT = NHARM * NBIN
-WIDE = 2048
+BOXES = 128
+BLK_DEV = 8
+Z_SIZE = 8
+PLANE = 16
+SOURCE_MOVES = (0, -1, 1, -2, 2, -3, 3, 4)
+PEERS = 2 * PLANE
+MESH = pl.DeviceIdType.MESH
 
 GROUPS = ((0, 1), (2, 3), (4, 5, 6), (7, 8, 9, 10))
-
-
-def padded(cells, sides, width):
-    for axis, dim in sides:
-        count = lax.axis_size(axis)
-        head = lax.slice_in_dim(cells, 0, width, axis=dim)
-        tail = lax.slice_in_dim(cells, cells.shape[dim] - width, cells.shape[dim], axis=dim)
-        cells = jnp.concatenate(
-            [
-                lax.ppermute(tail, axis, [(i, (i + 1) % count) for i in range(count)]),
-                cells,
-                lax.ppermute(head, axis, [((i + 1) % count, i) for i in range(count)]),
-            ],
-            axis=dim,
-        )
-    return cells
 
 
 def order_slices(degree_top, bin_count):
@@ -72,6 +62,103 @@
     return order_slices(LMAX, 1)[m_order][0]
 
 
+def near_kernel(counts_ref, pos_ref, weight_ref, region_ref, pool_ref, live_ref, code_ref, send, recv):
+    box, core = lax.axis_index("box"), lax.axis_index("help")
+    z_at, other = box // PLANE, 1 - core
+    above, below = (box + 1) % BOXES, (box + BOXES - 1) % BOXES
+    near = ((above, 0, 0), (above, 1, 0), (below, 0, 2), (below, 1, 2), (box, other, 1))
+    line = [((z_at + step) % Z_SIZE * PLANE + box % PLANE, core) for step in range(1, Z_SIZE)]
+    barrier = pltpu.get_barrier_semaphore()
+    for to_box, to_core, _ in near:
+        pl.semaphore_signal(barrier, inc=1, device_id=(to_box, to_core), device_id_type=MESH)
+    for target in line:
+        pl.semaphore_signal(barrier, inc=1, device_id=target, device_id_type=MESH)
+
+    lane = lax.broadcasted_iota(jnp.int32, (1, BS), 1)
+    mine = 2 + core
+    live = jnp.zeros((1, BS), jnp.int32)
+    for block in range(BLK_DEV):
+        count = counts_ref[block]
+        live = jnp.where(lane == block, count, live)
+        for axis in range(3):
+            pool_ref[mine, block, axis : axis + 1, :] = pos_ref[axis, block : block + 1, :]
+        pool_ref[mine, block, 3:4, :] = jnp.where(lane < count, weight_ref[block : block + 1, :], 0.0)
+        pool_ref[mine, block, 4:8, :] = jnp.zeros((4, BS), jnp.float32)
+    live_ref[mine] = live
+    row = lax.broadcasted_iota(jnp.int32, (PRIM_DEV, BS), 0)
+    col = lax.broadcasted_iota(jnp.int32, (PRIM_DEV, BS), 1)
+    over = jnp.concatenate([region_ref[...], jnp.zeros((1, BS - PRIM_DEV), jnp.int32)], axis=1)
+    down = jnp.sum(jnp.where(row == col, over, 0), axis=1, keepdims=True)
+    rank = jnp.sum(jnp.where((down == over) & (row < col), 1, 0), axis=0, keepdims=True)
+    code_ref[z_at] = jnp.where(lane < PRIM_DEV, 2 * over + rank, -1)
+
+    pl.semaphore_wait(barrier, 12)
+
+    def block_copy(slot, kind, target):
+        ref = (pool_ref, live_ref)[kind]
+        return pltpu.make_async_remote_copy(
+            src_ref=ref.at[mine],
+            dst_ref=ref.at[slot],
+            send_sem=send.at[slot, kind],
+            recv_sem=recv.at[slot, kind],
+            device_id=target,
+            device_id_type=MESH,
+        )
+
+    def code_copy(z_from, step):
+        return pltpu.make_async_remote_copy(
+            src_ref=code_ref.at[z_from],
+            dst_ref=code_ref.at[z_from],
+            send_sem=send.at[5 + step, 0],
+            recv_sem=recv.at[6 + z_from, 0],
+            device_id=line[step - 1],
+            device_id_type=MESH,
+        )
+
+    sends = []
+    for at, (to_box, to_core, move) in enumerate(near):
+        for kind in range(2):
+            ref = (pool_ref, live_ref)[kind]
+            sends.append(
+                pltpu.make_async_remote_copy(
+                    src_ref=ref.at[mine],
+                    dst_ref=ref.at[2 * move + core],
+                    send_sem=send.at[at, kind],
+                    recv_sem=recv.at[2 * move + core, kind],
+                    device_id=(to_box, to_core),
+                    device_id_type=MESH,
+                )
+            )
+    for step in range(1, Z_SIZE):
+        sends.append(code_copy(z_at, step))
+    for copy in sends:
+        copy.start()
+    for slot in (0, 1, 4, 5, 2 + other):
+        for kind in range(2):
+            block_copy(slot, kind, (box, other)).wait_recv()
+    for step in range(1, Z_SIZE):
+        code_copy((z_at + step) % Z_SIZE, step).wait_recv()
+    for copy in sends:
+        copy.wait_send()
+
+
+def near(counts, pos, weight, regions):
+    return pl.pallas_call(
+        near_kernel,
+        out_shape=(
+            jax.ShapeDtypeStruct((6, BLK_DEV, 8, BS), jnp.float32),
+            jax.ShapeDtypeStruct((6, 1, BS), jnp.int32),
+            jax.ShapeDtypeStruct((Z_SIZE, 1, BS), jnp.int32),
+        ),
+        in_specs=[pl.BlockSpec(memory_space=pltpu.SMEM)]
+        + [pl.BlockSpec(memory_space=pltpu.VMEM)] * 3,
+        out_specs=(pl.BlockSpec(memory_space=pltpu.VMEM),) * 3,
+        scratch_shapes=[pltpu.SemaphoreType.DMA((13, 2)), pltpu.SemaphoreType.DMA((14, 2))],
+        compiler_params=pltpu.CompilerParams(collective_id=0, has_side_effects=True),
+        name="near",
+    )(counts, pos, weight, regions)
+
+
 def turn_matrix():
     row = lax.broadcasted_iota(jnp.int32, (256, 256), 0)
     col = lax.broadcasted_iota(jnp.int32, (256, 256), 1)
@@ -79,37 +166,63 @@
 
 
 def pair_kernel(
-    pick_ref, count_ref, pool_ref, prim_ref, coef_ref, rows_ref, packed, basis, spline, acc, diag, spread
+    list_ref, pool_ref, live_ref, code_ref, pos_ref, weight_ref, coef_ref, rows_ref, table_ref,
+    packed, basis, spline, acc, diag, spread, live, sem
 ):
     tile = pl.program_id(0)
+    box, core = lax.axis_index("box"), lax.axis_index("help")
     lane = lax.broadcasted_iota(jnp.int32, (8, BS), 1)
 
     @pl.when(tile == 0)
     def _():
+        fetch = pltpu.make_async_copy(live_ref, live, sem)
+        fetch.start()
         row = lax.broadcasted_iota(jnp.int32, (PT * NBIN, 128), 0)
         col = lax.broadcasted_iota(jnp.int32, (PT * NBIN, 128), 1)
         for part in range(8):
             spread[part] = jnp.where(col == part * NBIN + row // PT, 1.0, 0.0).astype(jnp.bfloat16)
+        turn = lax.broadcasted_iota(jnp.int32, (2 * PEERS, BS), 0)
+        over = lax.broadcasted_iota(jnp.int32, (2 * PEERS, BS), 1)
+        x_to, y_to = (box // 4 + turn // 16) % 4, (box + turn // 4) % 4
+        owner = (box // PLANE * PLANE + x_to * 4 + y_to) * 2 + (core + turn // 2) % 2
+        wanted = owner * 2 + turn % 2
+        table = jnp.zeros((2 * PEERS, BS), jnp.int32)
+        for z_from in range(Z_SIZE):
+            found = jnp.max(
+                jnp.where(code_ref[z_from] == wanted, over, -1), axis=1, keepdims=True
+            )
+            table = jnp.where(over == z_from, found, table)
+        table_ref[...] = table
+        fetch.wait()
 
     packed[...] = jnp.zeros_like(packed)
     filled = jnp.int32(0)
     for slot in range(LIST):
-        pick = pick_ref[tile, slot]
-        block = pool_ref[jnp.maximum(pick, 0)]
+        listed = list_ref[tile, slot]
+        used = listed >= 0
+        listed = jnp.maximum(listed, 0)
+        owner = listed // BLK_DEV
+        place = jnp.where(used, (owner // 2 - box + 1 + BOXES) % BOXES * 2 + owner % 2, 0)
+        block = pool_ref[place, listed % BLK_DEV]
         base = filled // BS
         shift = filled % BS
         moved = pltpu.roll(block, shift, 1)
-        used = pick >= 0
         low = jnp.where((lane >= shift) & used, moved, packed[base])
         packed[base] = low
         high = jnp.where((lane < shift) & used, moved, packed[base + 1])
         packed[base + 1] = high
-        filled = filled + jnp.where(used, count_ref[jnp.maximum(pick, 0)], 0)
+        filled = filled + jnp.where(used, live[place, 0, listed % BLK_DEV], 0)
     chunks = (filled + 2 * BS - 1) // (2 * BS)
 
     acc[...] = jnp.zeros_like(acc)
-    prim = prim_ref[...]
-    px, py, pz = prim[:, 0:1], prim[:, 1:2], prim[:, 2:3]
+    own = lax.broadcasted_iota(jnp.int32, (PT, PRIM_DEV), 0) + tile * PT
+    own = own == lax.broadcasted_iota(jnp.int32, (PT, PRIM_DEV), 1)
+
+    def column(values):
+        return jnp.sum(jnp.where(own, values, 0.0), axis=1, keepdims=True)
+
+    px, py, pz = [column(pos_ref[axis : axis + 1, :]) for axis in range(3)]
+    scale_column = column(weight_ref[...]) * (1.0 / math.sqrt(LIST * BS))
     bin_step = 1.0 / (NBIN + 1)
 
     def chunk_step(chunk, carry):
@@ -196,7 +309,7 @@
 
     row = lax.broadcasted_iota(jnp.int32, (PT, PT * NBIN), 0)
     col = lax.broadcasted_iota(jnp.int32, (PT, PT * NBIN), 1)
-    keep = jnp.where(col % PT == row, prim[:, 3:4], 0.0)
+    keep = jnp.where(col % PT == row, scale_column, 0.0)
     for harm in range(128):
         if harm < NHARM:
             value = (acc[harm * PT : (harm + 1) * PT, :] * keep).astype(jnp.bfloat16)
@@ -214,24 +327,24 @@
     rows_ref[...] = turned.astype(jnp.bfloat16).reshape(PT, 16, 128)
 
 
-def pair_sums(pick, counts, pool, prim):
-    tiles = pick.shape[0]
+def pair_sums(lists, pool, live, codes, pos, weight):
+    tiles = lists.shape[0]
+    whole = pl.BlockSpec(memory_space=pltpu.VMEM)
     return pl.pallas_call(
         pair_kernel,
         out_shape=(
             jax.ShapeDtypeStruct((tiles * PT, FEAT), jnp.bfloat16),
             jax.ShapeDtypeStruct((tiles * PT, 16, 128), jnp.bfloat16),
+            jax.ShapeDtypeStruct((2 * PEERS, BS), jnp.int32),
         ),
         grid_spec=pltpu.PrefetchScalarGridSpec(
-            num_scalar_prefetch=2,
+            num_scalar_prefetch=1,
             grid=(tiles,),
-            in_specs=[
-                pl.BlockSpec(pool.shape, lambda t, *_: (0, 0, 0)),
-                pl.BlockSpec((PT, prim.shape[1]), lambda t, *_: (t, 0)),
-            ],
+            in_specs=[whole, pl.BlockSpec(memory_space=pl.ANY), whole, whole, whole],
             out_specs=(
                 pl.BlockSpec((PT, FEAT), lambda t, *_: (t, 0)),
                 pl.BlockSpec((PT, 16, 128), lambda t, *_: (t, 0, 0)),
+                pl.BlockSpec((2 * PEERS, BS), lambda t, *_: (0, 0)),
             ),
             scratch_shapes=[
                 pltpu.VMEM((2 * ((LIST + 1) // 2) + 2, 8, BS), jnp.float32),
@@ -240,18 +353,13 @@
                 pltpu.VMEM((NHARM * PT, NBIN * PT), jnp.float32),
                 pltpu.VMEM((8, 256, NBIN * PT), jnp.bfloat16),
                 pltpu.VMEM((8, NBIN * PT, 128), jnp.bfloat16),
+                pltpu.SMEM((6, 1, BS), jnp.int32),
+                pltpu.SemaphoreType.DMA(()),
             ],
         ),
         compiler_params=pltpu.CompilerParams(vmem_limit_bytes=40 << 20),
         name="pair_sums",
-    )(pick, counts, pool, prim)
-
-
-Z_SIZE = 8
-PLANE = 16
-SOURCE_MOVES = (0, -1, 1, -2, 2, -3, 3, 4)
-PEERS = 2 * PLANE
-MESH = pl.DeviceIdType.MESH
+    )(lists, pool, live, codes, pos, weight)
 
 
 def exchange_kernel(table_ref, rows_ref, out_ref, *scratch):
@@ -297,7 +405,7 @@
             for source in range(first, first + number):
                 z_from = (z_at + SOURCE_MOVES[source] + Z_SIZE) % Z_SIZE
                 for slot in range(2):
-                    row = table_ref[z_from * (2 * PEERS) + turn * 2 + slot]
+                    row = table_ref[turn * 2 + slot, z_from]
                     value = held[source][jnp.maximum(row, 0)]
                     target[turn, source, slot] = jnp.where(row >= 0, value, jnp.zeros_like(value))
 
@@ -367,24 +475,6 @@
         ),
         name="exchange",
     )(table, rows)
-
-
-def row_table(regions):
-    box, core = lax.axis_index("box"), lax.axis_index("help")
-    row_total = regions.shape[0]
-    row_order = jnp.arange(row_total, dtype=jnp.int32)
-    earlier = row_order[:, None] > row_order[None, :]
-    same_region = regions[:, None] == regions[None, :]
-    row_rank = jnp.sum((earlier & same_region).astype(jnp.int32), axis=1)
-    code = regions * 2 + row_rank
-    lines = [[at + PLANE * z for z in range(Z_SIZE)] for at in range(PLANE)]
-    codes = lax.all_gather(code, "box", axis_index_groups=lines)
-    turn = jnp.arange(PEERS, dtype=jnp.int32)
-    x_to, y_to = (box // 4 + turn // 8) % 4, (box + turn // 2) % 4
-    owner = (box // PLANE * PLANE + x_to * 4 + y_to) * 2 + (core + turn) % 2
-    wanted = (owner[:, None] * 2 + jnp.arange(2, dtype=jnp.int32)[None, :]).reshape(-1)
-    found = codes[:, None, :] == wanted[None, :, None]
-    return jnp.max(jnp.where(found, row_order[None, None, :], -1), axis=2).reshape(-1)
 
 
 def gram_kernel(rows_ref, out_ref, feats, gram):
@@ -476,36 +566,13 @@
 
 
 def shards(prim_pos, prim_weight, sec_pos, sec_weight, sec_counts, tile_lists, region_of):
-    box_count = lax.axis_size("box")
-    help_count = lax.axis_size("help")
-    per_device = sec_pos.shape[0]
-    lane_index = jnp.arange(sec_pos.shape[2], dtype=jnp.int32)
-    live_mask = (lane_index[None, :] < sec_counts[:, None]).astype(jnp.float32)
-    count_row = jnp.broadcast_to(
-        sec_counts.astype(jnp.float32)[:, None, None], (per_device, 4, sec_pos.shape[2])
+    pool, live, codes = near(
+        sec_counts, sec_pos.transpose(1, 0, 2), sec_weight, region_of.reshape(1, -1)
     )
-    own_blocks = jnp.concatenate(
-        [sec_pos, (sec_weight * live_mask)[:, None, :], count_row], axis=1
+    coefficients, rows, table = pair_sums(
+        tile_lists, pool, live, codes, prim_pos, prim_weight.reshape(1, -1)
     )
-    chip_pool = lax.all_gather(own_blocks, "help", axis=0, tiled=True)
-    block_pool = padded(chip_pool, (("box", 0),), chip_pool.shape[0])
-    pool_counts = block_pool[:, 4, 0].astype(jnp.int32)
-    in_use = tile_lists >= 0
-    safe_list = jnp.where(in_use, tile_lists, 0)
-    owner_dev = safe_list // per_device
-    box_move = jnp.mod(owner_dev // help_count - lax.axis_index("box") + 1, box_count)
-    pool_index = (
-        box_move * (help_count * per_device)
-        + owner_dev % help_count * per_device
-        + safe_list % per_device
-    )
-    pool_index = jnp.where(in_use, pool_index, -1).astype(jnp.int32)
-    row_total = prim_pos.shape[1]
-    norm_scale = 1.0 / math.sqrt(LIST * BS)
-    prim = jnp.concatenate([prim_pos, (prim_weight * norm_scale)[None, :]], axis=0).T
-
-    coefficients, rows = pair_sums(pool_index, pool_counts, block_pool, prim)
-    owner_rows = exchange(row_table(region_of[:, 0]), rows).reshape(-1, 16, 128)
+    owner_rows = exchange(table, rows).reshape(-1, 16, 128)
     region_tensor = gram_rows(owner_rows).reshape(1, -1)
     return (coefficients, region_tensor)
 

time: 101 us -> 87 us (0.86)
  blocking collectives: 15.8 us -> 0 us
  Pallas kernels: 66.6 us -> 80.4 us
  starting transfers between devices: 8.49 us -> 0 us
  other arithmetic: 6.39 us -> 0 us
  local copies, waits for them, and re-layouts: 2.4 us -> 5.61 us
    pallas_call x0 -> x1, Pallas kernels: none -> 17.8 us  [near(): pl.pallas_call(near_kernel, out_shape=(jax.ShapeDtypeStruct((6, BLK_DEV,...]
    all_gather x2 -> x0, blocking collectives: 15.8 us -> none  [the longest x1 11 us: row_table(): codes = lax.all_gather(code, 'box', axis_index_groups=lines)]
    ppermute x2 -> x0, starting transfers between devices: 8.49 us -> none  [the longest x1 8.49 us: padded(): lax.ppermute(head, axis, [((i + 1) % count, i) for i in range(count)])]
    pallas_call x1, Pallas kernels: 43.1 us -> 38.4 us  [exchange(): pl.pallas_call(exchange_kernel, out_shape=jax.ShapeDtypeStruct(shape, row...]
    unnamed x4 -> x13, local copies, waits for them, and re-layouts: 2.04 us -> 5.61 us
    convert_element_type x2 -> x0, other arithmetic: 1.6 us -> none  [the longest x1 0.94 us: shards(): pool_counts = block_pool[:, 4, 0].astype(jnp.int32)]
  transfers between devices with their start and end apart: 2 -> 0, of which waited for: 0 -> 0; matrix products, arithmetic and copies ran while one was open for 4% -> 0% of each run, Pallas kernels for 0% -> 0%
where the time goes in v3:
time: 87 us; the launch traced here: 86.7 us
  Pallas kernels  80.4 us (92%)
  local copies, waits for them, and re-layouts  5.61 us (6%)
    pallas_call x1, Pallas kernels, exchange(): pl.pallas_call(exchange_kernel, out_shape=jax.ShapeDtypeStruct(shape, row...  38.4 us
    pallas_call x1, Pallas kernels, near(): pl.pallas_call(near_kernel, out_shape=(jax.ShapeDtypeStruct((6, BLK_DEV,...  17.8 us
    pallas_call x1, Pallas kernels, pair_sums(): pl.pallas_call(pair_kernel, out_shape=(jax.ShapeDtypeStruct((tiles * PT,...  12.9 us
    pallas_call x1, Pallas kernels, gram_rows(): pl.pallas_call(gram_kernel, out_shape=jax.ShapeDtypeStruct((total // 128,...  11.3 us
    unnamed x13, local copies, waits for them, and re-layouts  5.61 us

profile of v3, /device:TPU:1, one launch (start us, length us, event | category | flops | bytes accessed | tf_op | source)
XLA Modules:
  0.0 86.7 jit_solution(8486893135470409402)
XLA Ops:
  0.6 17.8 %near.1 = (f32[6,8,8,128]{3,2,1,0:T(8,128)}, s32[6,1,128]{2,1,0:T(1,128)}, s32[8,1,128]{2,1,0:T(1,128)}) custom-call(s32[8]{0:T(128)} %counts_ref.1, f32[3,8,128]{2,1,0:T(8,128)} %bitcast.13, f32[8,128]{1,0:T(8,128)} %weight_ref.1, s32[1,64]{1,0:T(1,128)} %bitcast.14), custom_call_target="tpu_custom_call" | custom-call | tf_op jit(solution)/shard_map/near/pallas_call | solution.py:146
  18.4 0.0 copy-start
  18.4 0.9 %copy-done = f32[6,8,8,128]{3,2,1,0:T(8,128)S(1)} copy-done((f32[6,8,8,128]{3,2,1,0:T(8,128)S(1)}, f32[6,8,8,128]{3,2,1,0:T(8,128)}, u32[]{:S(2)}) %copy-start) | copy-done | bytes 196632
  19.3 0.0 copy-start.1
  19.4 0.7 copy-done.1
  20.0 0.0 copy-start.2
  20.0 0.7 copy-done.2
  20.7 0.0 copy-start.3
  20.7 0.7 copy-done.3
  21.4 0.0 copy-start.4
  21.4 0.7 copy-done.4
  22.1 0.0 copy-start.5
  22.1 0.7 copy-done.5
  22.7 12.9 %pair_sums.1 = (bf16[64,1936]{1,0:T(8,128)(2,1)}, bf16[64,16,128]{2,1,0:T(8,128)(2,1)S(1)}, s32[64,128]{1,0:T(8,128)S(1)}) custom-call(s32[4,12]{1,0:T(4,128)S(1)} %copy-done.3, f32[6,8,8,128]{3,2,1,0:T(8,128)S(1)} %copy-done, s32[6,1,128]{2,1,0:T(1,128)S(1)} %copy-done.2, s32[8,1,128]{2,1,0:T(1,128)S(1)} %copy-done.1, f32[3,64]{1,0:T(4,128)S(1)} %copy-done.4, ...), custom_call_target="tpu_custom_call" | custom-call | tf_op jit(solution)/shard_map/pair_sums/pallas_call | solution.py:333
  35.6 38.4 %exchange.1 = bf16[32,8,2,16,128]{4,3,2,1,0:T(8,128)(2,1)S(1)} custom-call(s32[64,128]{1,0:T(8,128)S(1)} %get-tuple-element.12.table_ref, bf16[64,16,128]{2,1,0:T(8,128)(2,1)S(1)} %get-tuple-element.13.rows_ref), custom_call_target="tpu_custom_call" | custom-call | tf_op jit(solution)/shard_map/exchange/pallas_call | solution.py:457
  74.0 11.3 %gram_rows.1 = f32[1012,128]{1,0:T(8,128)S(1)} custom-call(bf16[512,16,128]{2,1,0:T(8,128)(2,1)S(1)} %bitcast.9), custom_call_target="tpu_custom_call" | custom-call | tf_op jit(solution)/shard_map/gram_rows/pallas_call | solution.py:554
  85.4 1.3 %copy.11 = f32[1,1,1012,128]{3,1,2,0:T(1,128)} copy(f32[1,1,1012,128]{3,2,1,0:T(8,128)S(1)} %bitcast.10) | data formatting | bytes 1036288
Async XLA Ops:
  18.4 0.9 %copy-start = (f32[6,8,8,128]{3,2,1,0:T(8,128)S(1)}, f32[6,8,8,128]{3,2,1,0:T(8,128)}, u32[]{:S(2)}) copy-start(f32[6,8,8,128]{3,2,1,0:T(8,128)} %get-tuple-element.8.pool_ref) | copy-start | bytes 589828
  19.3 0.7 copy-start.1
  20.0 0.7 copy-start.2
  20.7 0.7 copy-start.3
  21.4 0.7 copy-start.4
  22.1 0.7 copy-start.5

commit v4 on v3

--- a/solution.py
+++ b/solution.py
@@ -154,7 +154,9 @@
         + [pl.BlockSpec(memory_space=pltpu.VMEM)] * 3,
         out_specs=(pl.BlockSpec(memory_space=pltpu.VMEM),) * 3,
         scratch_shapes=[pltpu.SemaphoreType.DMA((13, 2)), pltpu.SemaphoreType.DMA((14, 2))],
-        compiler_params=pltpu.CompilerParams(collective_id=0, has_side_effects=True),
+        compiler_params=pltpu.CompilerParams(
+            collective_id=0, has_side_effects=True, vmem_limit_bytes=8 << 20
+        ),
         name="near",
     )(counts, pos, weight, regions)
 
@@ -166,8 +168,8 @@
 
 
 def pair_kernel(
-    list_ref, pool_ref, live_ref, code_ref, pos_ref, weight_ref, coef_ref, rows_ref, table_ref,
-    packed, basis, spline, acc, diag, spread, live, sem
+    list_ref, pool_hbm, live_hbm, code_hbm, pos_hbm, weight_hbm, coef_ref, rows_ref, table_ref,
+    packed, basis, spline, acc, diag, spread, pool_ref, live, code_ref, pos_ref, weight_ref, sem
 ):
     tile = pl.program_id(0)
     box, core = lax.axis_index("box"), lax.axis_index("help")
@@ -175,12 +177,26 @@
 
     @pl.when(tile == 0)
     def _():
-        fetch = pltpu.make_async_copy(live_ref, live, sem)
-        fetch.start()
+        fetches = [
+            pltpu.make_async_copy(source, target, sem.at[at])
+            for at, (source, target) in enumerate(
+                (
+                    (pool_hbm, pool_ref),
+                    (live_hbm, live),
+                    (code_hbm, code_ref),
+                    (pos_hbm, pos_ref),
+                    (weight_hbm, weight_ref),
+                )
+            )
+        ]
+        for fetch in fetches:
+            fetch.start()
         row = lax.broadcasted_iota(jnp.int32, (PT * NBIN, 128), 0)
         col = lax.broadcasted_iota(jnp.int32, (PT * NBIN, 128), 1)
         for part in range(8):
             spread[part] = jnp.where(col == part * NBIN + row // PT, 1.0, 0.0).astype(jnp.bfloat16)
+        for fetch in fetches:
+            fetch.wait()
         turn = lax.broadcasted_iota(jnp.int32, (2 * PEERS, BS), 0)
         over = lax.broadcasted_iota(jnp.int32, (2 * PEERS, BS), 1)
         x_to, y_to = (box // 4 + turn // 16) % 4, (box + turn // 4) % 4
@@ -193,7 +209,6 @@
             )
             table = jnp.where(over == z_from, found, table)
         table_ref[...] = table
-        fetch.wait()
 
     packed[...] = jnp.zeros_like(packed)
     filled = jnp.int32(0)
@@ -329,7 +344,7 @@
 
 def pair_sums(lists, pool, live, codes, pos, weight):
     tiles = lists.shape[0]
-    whole = pl.BlockSpec(memory_space=pltpu.VMEM)
+    operands = (pool, live, codes, pos, weight)
     return pl.pallas_call(
         pair_kernel,
         out_shape=(
@@ -340,7 +355,7 @@
         grid_spec=pltpu.PrefetchScalarGridSpec(
             num_scalar_prefetch=1,
             grid=(tiles,),
-            in_specs=[whole, pl.BlockSpec(memory_space=pl.ANY), whole, whole, whole],
+            in_specs=[pl.BlockSpec(memory_space=pltpu.HBM)] * len(operands),
             out_specs=(
                 pl.BlockSpec((PT, FEAT), lambda t, *_: (t, 0)),
                 pl.BlockSpec((PT, 16, 128), lambda t, *_: (t, 0, 0)),
@@ -353,18 +368,60 @@
                 pltpu.VMEM((NHARM * PT, NBIN * PT), jnp.float32),
                 pltpu.VMEM((8, 256, NBIN * PT), jnp.bfloat16),
                 pltpu.VMEM((8, NBIN * PT, 128), jnp.bfloat16),
-                pltpu.SMEM((6, 1, BS), jnp.int32),
-                pltpu.SemaphoreType.DMA(()),
+                pltpu.VMEM(pool.shape, pool.dtype),
+                pltpu.SMEM(live.shape, live.dtype),
+                pltpu.VMEM(codes.shape, codes.dtype),
+                pltpu.VMEM(pos.shape, pos.dtype),
+                pltpu.VMEM(weight.shape, weight.dtype),
+                pltpu.SemaphoreType.DMA((len(operands),)),
             ],
         ),
         compiler_params=pltpu.CompilerParams(vmem_limit_bytes=40 << 20),
         name="pair_sums",
-    )(lists, pool, live, codes, pos, weight)
-
-
-def exchange_kernel(table_ref, rows_ref, out_ref, *scratch):
+    )(lists, *operands)
+
+
+def gram_tiles():
+    tiles = []
+    for m_order, (cos_start, sin_start, length) in enumerate(order_slices(LMAX, NBIN)):
+        for kind, start in enumerate((cos_start, sin_start)):
+            if start >= 0:
+                for part in range(-(-length // 128)):
+                    width = min(128, length - 128 * part)
+                    tiles.append((m_order, kind, start + 128 * part, width))
+    return tiles
+
+
+def gram_flatten(gram, out_ref, base, count):
+    lane = lax.broadcasted_iota(jnp.int32, (2 * count, 128), 1)
+    for rest in range(8):
+        for part in range(-(-count // 8)):
+            units = min(8, count - 8 * part)
+            shift = rest * count % 8
+            at = base + rest * count // 8 + part
+            value = gram[part, pl.ds(rest, 2 * count, stride=8), :] * (1.0 / PRIM_DEV)
+            if shift:
+                value = pltpu.roll(value, 16 * shift, 1)
+            window = pl.ds(at, 2 * count, stride=count)
+            keep = (lane >= 16 * shift) & (lane < 16 * (shift + units))
+            out_ref[window, :] = jnp.where(keep, value, out_ref[window, :])
+            if shift + units > 8:
+                window = pl.ds(at + 1, 2 * count, stride=count)
+                keep = lane < 16 * (shift + units - 8)
+                out_ref[window, :] = jnp.where(keep, value, out_ref[window, :])
+
+
+PLANE_MOVES = (
+    (1, 0), (3, 0), (0, 1), (0, 3), (1, 1), (3, 3), (1, 3), (3, 1),
+    (2, 0), (0, 2), (2, 2), (2, 1), (1, 2), (2, 3), (3, 2),
+)
+BATCHES = ((0, 1), (1, 2), (3, 2), (5, 2), (7, 1))
+
+
+def regions_kernel(table_ref, rows_ref, out_ref, *scratch):
     held = (rows_ref,) + scratch[:7]
-    stage, ring_send, ring_recv, plane_send, plane_recv = scratch[7:]
+    stage, come, feats, shifts, plain, flipped, gram = scratch[7:14]
+    ring_send, ring_recv, plane_send, plane_recv = scratch[14:]
     box, core = lax.axis_index("box"), lax.axis_index("help")
     z_at, x_at, y_at = box // PLANE, (box // 4) % 4, box % 4
     ring = (
@@ -400,7 +457,9 @@
             device_id_type=MESH,
         )
 
-    def deal(batch, first, number):
+    def deal(batch):
+        first, number = BATCHES[batch]
+
         def fill(turn, target):
             for source in range(first, first + number):
                 z_from = (z_at + SOURCE_MOVES[source] + Z_SIZE) % Z_SIZE
@@ -409,54 +468,128 @@
                     value = held[source][jnp.maximum(row, 0)]
                     target[turn, source, slot] = jnp.where(row >= 0, value, jnp.zeros_like(value))
 
-        fill(0, out_ref)
-
-        def one_peer(count, carry):
-            turn = count * 13 % PEERS
+        def one_peer(turn):
             fill(turn, stage)
             pltpu.make_async_remote_copy(
                 src_ref=stage.at[turn, pl.ds(first, number)],
-                dst_ref=out_ref.at[turn, pl.ds(first, number)],
+                dst_ref=come.at[turn, pl.ds(first, number)],
                 send_sem=plane_send.at[batch],
                 recv_sem=plane_recv.at[batch],
                 device_id=peer(turn),
                 device_id_type=MESH,
             ).start()
+
+        def one_core(core_move, carry):
+            for x_move, y_move in PLANE_MOVES:
+                one_peer(x_move * 8 + y_move * 2 + core_move)
             return carry
 
-        lax.fori_loop(1, PEERS, one_peer, 0)
+        lax.fori_loop(0, 2, one_core, 0)
+        one_peer(1)
+        fill(0, come)
+
+    tiles = gram_tiles()
+    across = (((1,), (1,)), ((), ()))
+
+    def prepare():
+        row = lax.broadcasted_iota(jnp.int32, (128, 128), 0)
+        col = lax.broadcasted_iota(jnp.int32, (128, 128), 1)
+        for unit in range(-7, 8):
+            hit = row == col + 16 * unit
+            shifts[unit + 7] = jnp.where(hit, 1.0, 0.0).astype(jnp.bfloat16)
+
+    def collect(batch):
+        first, number = BATCHES[batch]
+        arrived = come.at[pl.ds(1, PEERS - 1), pl.ds(first, number)]
+        pltpu.make_async_copy(arrived, arrived, plane_recv.at[batch]).wait()
+        turn = turn_matrix()
+        for source in range(number):
+
+            def regroup(step, carry, source=source):
+                block = come[pl.ds(step * 8, 8), first + source].reshape(256, 128)
+                moved = jnp.dot(turn, block, preferred_element_type=jnp.float32)
+                at = pl.multiple_of(source * 64 + step * 16, 16)
+                feats[:, pl.ds(at, 16), :] = moved.astype(jnp.bfloat16).reshape(16, 16, 128)
+                return carry
+
+            lax.fori_loop(0, 4, regroup, 0, unroll=True)
+        size = 64 * number
+        at = (384, 0, 128, 256, 448)[batch]
+        for tile, (_, _, start, width) in enumerate(tiles):
+            group, skip = start // 128, start % 128 // 16
+            here = feats[group, 0:size, :]
+            over = lax.dot_general(
+                shifts[7 - skip], here, across, preferred_element_type=jnp.float32
+            )
+            if skip == 0:
+                down = here
+            else:
+                down = jnp.dot(here, shifts[7 + skip], preferred_element_type=jnp.float32)
+                if skip * 16 + width > 128:
+                    there = feats[group + 1, 0:size, :]
+                    down += jnp.dot(there, shifts[skip - 1], preferred_element_type=jnp.float32)
+                    over += lax.dot_general(
+                        shifts[15 - skip], there, across, preferred_element_type=jnp.float32
+                    )
+            plain[tile, at : at + size, :] = down.astype(jnp.bfloat16)
+            flipped[tile, :, at : at + size] = over.astype(jnp.bfloat16)
 
     for half in range(2):
         for way in range(2):
             ring_copy(way, 1, half).start()
-    deal(0, 0, 1)
+    deal(0)
+    prepare()
     for step in range(1, 4):
         for half in range(2):
             for way in range(2):
                 ring_copy(way, step, half).wait_recv()
                 if step < 3 or half == way:
                     ring_copy(way, step + 1, half).start()
-        deal(step, 2 * step - 1, 2)
+            if half == 0 and step > 1:
+                collect(step - 2)
+        deal(step)
     for way in range(2):
         ring_copy(way, 4, way).wait_recv()
-    deal(4, 7, 1)
+    deal(4)
+    for batch in range(2, 5):
+        collect(batch)
+
+    base = 0
+    for m_order, (_, _, length) in enumerate(order_slices(LMAX, NBIN)):
+        parts = -(-length // 128)
+        for kind in range(2):
+            mine = [at for at, tile in enumerate(tiles) if tile[:2] == (m_order, kind)]
+            for up, up_tile in enumerate(mine):
+                for over, over_tile in enumerate(mine):
+                    product = jnp.dot(
+                        flipped[up_tile], plain[over_tile], preferred_element_type=jnp.float32
+                    )
+                    at = (over, slice(up * 128, up * 128 + 128))
+                    if kind == 0:
+                        gram[at] = product
+                    else:
+                        gram[at] += product
+        gram_flatten(gram, out_ref, base, length // NBIN)
+        base += length * length // 128
+
     for step in range(1, 5):
         for half in range(2):
             for way in range(2):
                 if step < 4 or half == way:
                     ring_copy(way, step, half).wait_send()
-    for batch, first, number in ((0, 0, 1), (1, 1, 2), (2, 3, 2), (3, 5, 2), (4, 7, 1)):
+    for batch, (first, number) in enumerate(BATCHES):
         sent = stage.at[pl.ds(1, PEERS - 1), pl.ds(first, number)]
         pltpu.make_async_copy(sent, sent, plane_send.at[batch]).wait()
-        come = out_ref.at[pl.ds(1, PEERS - 1), pl.ds(first, number)]
-        pltpu.make_async_copy(come, come, plane_recv.at[batch]).wait()
-
-
-def exchange(table, rows):
+
+
+def region_products(table, rows):
     shape = (PEERS, Z_SIZE, 2, 16, 128)
+    total = sum(length * length for _, _, length in order_slices(LMAX, NBIN))
+    tiles = len(gram_tiles())
+    row_total = PEERS * Z_SIZE * 2
     return pl.pallas_call(
-        exchange_kernel,
-        out_shape=jax.ShapeDtypeStruct(shape, rows.dtype),
+        regions_kernel,
+        out_shape=jax.ShapeDtypeStruct((total // 128, 128), jnp.float32),
         in_specs=[
             pl.BlockSpec(memory_space=pltpu.SMEM),
             pl.BlockSpec(memory_space=pltpu.VMEM),
@@ -465,6 +598,12 @@
         scratch_shapes=[pltpu.VMEM(rows.shape, rows.dtype)] * 7
         + [
             pltpu.VMEM(shape, rows.dtype),
+            pltpu.VMEM(shape, rows.dtype),
+            pltpu.VMEM((16, 128, 128), rows.dtype),
+            pltpu.VMEM((15, 128, 128), rows.dtype),
+            pltpu.VMEM((tiles, row_total, 128), rows.dtype),
+            pltpu.VMEM((tiles, 128, row_total), rows.dtype),
+            pltpu.VMEM((2, 256, 128), jnp.float32),
             pltpu.SemaphoreType.DMA((2, 4, 2)),
             pltpu.SemaphoreType.DMA((2, 4, 2)),
             pltpu.SemaphoreType.DMA((5,)),
@@ -473,96 +612,8 @@
         compiler_params=pltpu.CompilerParams(
             collective_id=1, has_side_effects=True, vmem_limit_bytes=40 << 20
         ),
-        name="exchange",
+        name="region_products",
     )(table, rows)
-
-
-def gram_kernel(rows_ref, out_ref, feats, gram):
-    row_total = rows_ref.shape[0]
-    turn = turn_matrix()
-
-    def regroup(step, carry):
-        at = pl.multiple_of(step * 16, 16)
-        block = rows_ref[pl.ds(at, 16)].reshape(256, 128)
-        moved = jnp.dot(turn, block, preferred_element_type=jnp.float32).astype(jnp.bfloat16)
-        feats[:, pl.ds(at, 16), :] = moved.reshape(16, 16, 128)
-        return carry
-
-    lax.fori_loop(0, row_total // 16, regroup, 0)
-    row = lax.broadcasted_iota(jnp.int32, (128, 128), 0)
-    col = lax.broadcasted_iota(jnp.int32, (128, 128), 1)
-
-    def one_hot(cond):
-        return jnp.where(cond, 1.0, 0.0).astype(jnp.bfloat16)
-
-    def aligned(start, width):
-        group, skip = start // 128, start % 128
-        here, there = one_hot(row == col + skip), one_hot(row + 128 == col + skip)
-        here_t, there_t = one_hot(col == row + skip), one_hot(col + 128 == row + skip)
-        across = (((1,), (1,)), ((), ()))
-        plain = jnp.dot(feats[group], here, preferred_element_type=jnp.float32)
-        flipped = lax.dot_general(here_t, feats[group], across, preferred_element_type=jnp.float32)
-        if skip + width > 128:
-            plain += jnp.dot(feats[group + 1], there, preferred_element_type=jnp.float32)
-            flipped += lax.dot_general(
-                there_t, feats[group + 1], across, preferred_element_type=jnp.float32
-            )
-        return plain.astype(jnp.bfloat16), flipped.astype(jnp.bfloat16)
-
-    base = 0
-    for cos_start, sin_start, length in order_slices(LMAX, NBIN):
-        count = length // NBIN
-        parts = -(-length // 128)
-        for kind_start in (cos_start, sin_start):
-            if kind_start < 0:
-                continue
-            tiles = [
-                aligned(kind_start + 128 * part, min(128, length - 128 * part))
-                for part in range(parts)
-            ]
-            for up in range(parts):
-                for over in range(parts):
-                    product = jnp.dot(
-                        tiles[up][1], tiles[over][0], preferred_element_type=jnp.float32
-                    )
-                    at = (over, slice(up * 128, up * 128 + 128))
-                    if kind_start == cos_start:
-                        gram[at] = product
-                    else:
-                        gram[at] += product
-        lane = lax.broadcasted_iota(jnp.int32, (2 * count, 128), 1)
-        for rest in range(8):
-            for part in range(parts):
-                units = min(8, count - 8 * part)
-                shift = rest * count % 8
-                at = base + rest * count // 8 + part
-                value = gram[part, pl.ds(rest, 2 * count, stride=8), :] * (1.0 / PRIM_DEV)
-                if shift:
-                    value = pltpu.roll(value, 16 * shift, 1)
-                window = pl.ds(at, 2 * count, stride=count)
-                keep = (lane >= 16 * shift) & (lane < 16 * (shift + units))
-                out_ref[window, :] = jnp.where(keep, value, out_ref[window, :])
-                if shift + units > 8:
-                    window = pl.ds(at + 1, 2 * count, stride=count)
-                    keep = lane < 16 * (shift + units - 8)
-                    out_ref[window, :] = jnp.where(keep, value, out_ref[window, :])
-        base += 2 * count * count
-
-
-def gram_rows(rows):
-    total = sum(length * length for _, _, length in order_slices(LMAX, NBIN))
-    return pl.pallas_call(
-        gram_kernel,
-        out_shape=jax.ShapeDtypeStruct((total // 128, 128), jnp.float32),
-        in_specs=[pl.BlockSpec(memory_space=pltpu.VMEM)],
-        out_specs=pl.BlockSpec(memory_space=pltpu.VMEM),
-        scratch_shapes=[
-            pltpu.VMEM((16, rows.shape[0], 128), jnp.bfloat16),
-            pltpu.VMEM((2, 256, 128), jnp.float32),
-        ],
-        compiler_params=pltpu.CompilerParams(vmem_limit_bytes=40 << 20),
-        name="gram_rows",
-    )(rows)
 
 
 def shards(prim_pos, prim_weight, sec_pos, sec_weight, sec_counts, tile_lists, region_of):
@@ -572,8 +623,7 @@
     coefficients, rows, table = pair_sums(
         tile_lists, pool, live, codes, prim_pos, prim_weight.reshape(1, -1)
     )
-    owner_rows = exchange(table, rows).reshape(-1, 16, 128)
-    region_tensor = gram_rows(owner_rows).reshape(1, -1)
+    region_tensor = region_products(table, rows).reshape(1, -1)
     return (coefficients, region_tensor)
 
 

time: 87 us -> 75.2 us (0.86)
  Pallas kernels: 80.4 us -> 70.8 us
  local copies, waits for them, and re-layouts: 5.61 us -> 3.37 us
    pallas_call x2 -> x1, Pallas kernels: 49.8 us -> 40.7 us  [region_products(): pl.pallas_call(regions_kernel, out_shape=jax.ShapeDtypeStruct((total // 1...]
    unnamed x13 -> x15, local copies, waits for them, and re-layouts: 5.61 us -> 3.37 us
    pallas_call x1, Pallas kernels: 17.8 us -> 16.7 us  [near(): pl.pallas_call(near_kernel, out_shape=(jax.ShapeDtypeStruct((6, BLK_DEV,...]
where the time goes in v4:
time: 75.2 us; the launch traced here: 74.9 us
  Pallas kernels  70.8 us (94%)
  local copies, waits for them, and re-layouts  3.37 us (4%)
    pallas_call x1, Pallas kernels, region_products(): pl.pallas_call(regions_kernel, out_shape=jax.ShapeDtypeStruct((total // 1...  40.7 us
    pallas_call x1, Pallas kernels, near(): pl.pallas_call(near_kernel, out_shape=(jax.ShapeDtypeStruct((6, BLK_DEV,...  16.7 us
    pallas_call x1, Pallas kernels, pair_sums(): pl.pallas_call(pair_kernel, out_shape=(jax.ShapeDtypeStruct((tiles * PT,...  13.5 us
    unnamed x15, local copies, waits for them, and re-layouts  3.37 us

profile of v4, /device:TPU:1, one launch (start us, length us, event | category | flops | bytes accessed | tf_op | source)
XLA Modules:
  0.0 74.9 jit_solution(16271741738669940068)
XLA Ops:
  0.6 0.0 copy-start.1
  0.6 0.0 copy-start.5
  0.7 0.0 copy-start.6
  0.7 0.7 copy-done.1
  1.3 0.0 copy-done.5
  1.3 0.0 copy-done.6
  1.3 0.0 copy-start
  1.3 0.7 copy-done
  2.0 16.7 %near.1 = (f32[6,8,8,128]{3,2,1,0:T(8,128)S(1)}, s32[6,1,128]{2,1,0:T(1,128)S(1)}, s32[8,1,128]{2,1,0:T(1,128)S(1)}) custom-call(s32[8]{0:T(128)S(1)} %copy-done.5, f32[3,8,128]{2,1,0:T(8,128)S(1)} %bitcast.9, f32[8,128]{1,0:T(8,128)S(1)} %copy-done.1, s32[1,64]{1,0:T(1,128)S(1)} %bitcast.11), custom_call_target="tpu_custom_call" | custom-call | tf_op jit(solution)/shard_map/near/pallas_call | solution.py:146
  18.7 0.0 copy-start.3
  18.8 0.0 copy-start.2
  18.8 0.0 copy-start.4
  18.8 0.6 copy-done.3
  19.4 0.0 copy-done.2
  19.4 0.0 copy-done.4
  19.5 13.5 %pair_sums.1 = (bf16[64,1936]{1,0:T(8,128)(2,1)}, bf16[64,16,128]{2,1,0:T(8,128)(2,1)S(1)}, s32[64,128]{1,0:T(8,128)S(1)}) custom-call(s32[4,12]{1,0:T(4,128)S(1)} %copy-done.2, f32[6,8,8,128]{3,2,1,0:T(8,128)S(1)} %get-tuple-element.8.pool_hbm, s32[6,1,128]{2,1,0:T(1,128)S(1)} %get-tuple-element.9.live_hbm, s32[8,1,128]{2,1,0:T(1,128)S(1)} %get-tuple-element.10.code_hbm, ...), custom_call_target="tpu_custom_call" | custom-call | tf_op jit(solution)/shard_map/pair_sums/pallas_call | solution.py:348
  32.9 40.7 %region_products.1 = f32[1012,128]{1,0:T(8,128)S(1)} custom-call(s32[64,128]{1,0:T(8,128)S(1)} %get-tuple-element.12.table_ref, bf16[64,16,128]{2,1,0:T(8,128)(2,1)S(1)} %get-tuple-element.13.rows_ref), custom_call_target="tpu_custom_call" | custom-call | tf_op jit(solution)/shard_map/region_products/pallas_call | solution.py:590
  73.6 1.3 %copy.11 = f32[1,1,1012,128]{3,1,2,0:T(1,128)} copy(f32[1,1,1012,128]{3,2,1,0:T(8,128)S(1)} %bitcast.8) | data formatting | bytes 1036288
Async XLA Ops:
  0.6 0.7 copy-start.1
  0.6 0.7 copy-start.5
  0.7 0.7 copy-start.6
  1.3 0.7 copy-start
  18.7 0.7 copy-start.3
  18.8 0.7 copy-start.2
  18.8 0.7 copy-start.4

commit v5 on v4

--- a/solution.py
+++ b/solution.py
@@ -24,7 +24,7 @@
 PEERS = 2 * PLANE
 MESH = pl.DeviceIdType.MESH
 
-GROUPS = ((0, 1), (2, 3), (4, 5, 6), (7, 8, 9, 10))
+GROUPS = ((0, 1, 2, 3, 4, 5, 6, 7, 8, 9, 10),)
 
 
 def order_slices(degree_top, bin_count):
@@ -62,7 +62,16 @@
     return order_slices(LMAX, 1)[m_order][0]
 
 
-def near_kernel(counts_ref, pos_ref, weight_ref, region_ref, pool_ref, live_ref, code_ref, send, recv):
+def turn_matrix():
+    row = lax.broadcasted_iota(jnp.int32, (256, 256), 0)
+    col = lax.broadcasted_iota(jnp.int32, (256, 256), 1)
+    return jnp.where(col == (row % 16) * 16 + row // 16, 1.0, 0.0).astype(jnp.bfloat16)
+
+
+def near_kernel(
+    counts_ref, pos_ref, weight_ref, region_ref,
+    pool_ref, live_ref, code_ref, spread_ref, turn_ref, send, recv
+):
     box, core = lax.axis_index("box"), lax.axis_index("help")
     z_at, other = box // PLANE, 1 - core
     above, below = (box + 1) % BOXES, (box + BOXES - 1) % BOXES
@@ -133,6 +142,12 @@
         sends.append(code_copy(z_at, step))
     for copy in sends:
         copy.start()
+    row = lax.broadcasted_iota(jnp.int32, (128, 128), 0)
+    col = lax.broadcasted_iota(jnp.int32, (128, 128), 1)
+    for part in range(8):
+        hit = col - part * NBIN == row // 8
+        spread_ref[part] = jnp.where(hit, 1.0, 0.0).astype(jnp.bfloat16)
+    turn_ref[...] = turn_matrix()
     for slot in (0, 1, 4, 5, 2 + other):
         for kind in range(2):
             block_copy(slot, kind, (box, other)).wait_recv()
@@ -149,10 +164,12 @@
             jax.ShapeDtypeStruct((6, BLK_DEV, 8, BS), jnp.float32),
             jax.ShapeDtypeStruct((6, 1, BS), jnp.int32),
             jax.ShapeDtypeStruct((Z_SIZE, 1, BS), jnp.int32),
+            jax.ShapeDtypeStruct((8, 128, 128), jnp.bfloat16),
+            jax.ShapeDtypeStruct((256, 256), jnp.bfloat16),
         ),
         in_specs=[pl.BlockSpec(memory_space=pltpu.SMEM)]
         + [pl.BlockSpec(memory_space=pltpu.VMEM)] * 3,
-        out_specs=(pl.BlockSpec(memory_space=pltpu.VMEM),) * 3,
+        out_specs=(pl.BlockSpec(memory_space=pltpu.VMEM),) * 5,
         scratch_shapes=[pltpu.SemaphoreType.DMA((13, 2)), pltpu.SemaphoreType.DMA((14, 2))],
         compiler_params=pltpu.CompilerParams(
             collective_id=0, has_side_effects=True, vmem_limit_bytes=8 << 20
@@ -161,15 +178,9 @@
     )(counts, pos, weight, regions)
 
 
-def turn_matrix():
-    row = lax.broadcasted_iota(jnp.int32, (256, 256), 0)
-    col = lax.broadcasted_iota(jnp.int32, (256, 256), 1)
-    return jnp.where(col == (row % 16) * 16 + row // 16, 1.0, 0.0).astype(jnp.bfloat16)
-
-
 def pair_kernel(
-    list_ref, pool_hbm, live_hbm, code_hbm, pos_hbm, weight_hbm, coef_ref, rows_ref, table_ref,
-    packed, basis, spline, acc, diag, spread, pool_ref, live, code_ref, pos_ref, weight_ref, sem
+    list_ref, pool_ref, live_ref, code_ref, pos_ref, weight_ref, spread, turn_ref,
+    coef_ref, rows_ref, table_ref, packed, basis, spline, acc, diag, live, sem
 ):
     tile = pl.program_id(0)
     box, core = lax.axis_index("box"), lax.axis_index("help")
@@ -177,26 +188,8 @@
 
     @pl.when(tile == 0)
     def _():
-        fetches = [
-            pltpu.make_async_copy(source, target, sem.at[at])
-            for at, (source, target) in enumerate(
-                (
-                    (pool_hbm, pool_ref),
-                    (live_hbm, live),
-                    (code_hbm, code_ref),
-                    (pos_hbm, pos_ref),
-                    (weight_hbm, weight_ref),
-                )
-            )
-        ]
-        for fetch in fetches:
-            fetch.start()
-        row = lax.broadcasted_iota(jnp.int32, (PT * NBIN, 128), 0)
-        col = lax.broadcasted_iota(jnp.int32, (PT * NBIN, 128), 1)
-        for part in range(8):
-            spread[part] = jnp.where(col == part * NBIN + row // PT, 1.0, 0.0).astype(jnp.bfloat16)
-        for fetch in fetches:
-            fetch.wait()
+        fetch = pltpu.make_async_copy(live_ref, live, sem)
+        fetch.start()
         turn = lax.broadcasted_iota(jnp.int32, (2 * PEERS, BS), 0)
         over = lax.broadcasted_iota(jnp.int32, (2 * PEERS, BS), 1)
         x_to, y_to = (box // 4 + turn // 16) % 4, (box + turn // 4) % 4
@@ -209,6 +202,7 @@
             )
             table = jnp.where(over == z_from, found, table)
         table_ref[...] = table
+        fetch.wait()
 
     packed[...] = jnp.zeros_like(packed)
     filled = jnp.int32(0)
@@ -216,18 +210,18 @@
         listed = list_ref[tile, slot]
         used = listed >= 0
         listed = jnp.maximum(listed, 0)
-        owner = listed // BLK_DEV
-        place = jnp.where(used, (owner // 2 - box + 1 + BOXES) % BOXES * 2 + owner % 2, 0)
-        block = pool_ref[place, listed % BLK_DEV]
-        base = filled // BS
-        shift = filled % BS
+        owner, inner = listed >> 3, listed & (BLK_DEV - 1)
+        place = jnp.where(used, (((owner >> 1) - box + 1) & (BOXES - 1)) * 2 + (owner & 1), 0)
+        block = pool_ref[place, inner]
+        base = filled >> 7
+        shift = filled & (BS - 1)
         moved = pltpu.roll(block, shift, 1)
         low = jnp.where((lane >= shift) & used, moved, packed[base])
         packed[base] = low
         high = jnp.where((lane < shift) & used, moved, packed[base + 1])
         packed[base + 1] = high
-        filled = filled + jnp.where(used, live[place, 0, listed % BLK_DEV], 0)
-    chunks = (filled + 2 * BS - 1) // (2 * BS)
+        filled = filled + jnp.where(used, live[place, 0, inner], 0)
+    chunks = (filled + 2 * BS - 1) >> 8
 
     acc[...] = jnp.zeros_like(acc)
     own = lax.broadcasted_iota(jnp.int32, (PT, PRIM_DEV), 0) + tile * PT
@@ -258,12 +252,17 @@
             lower = weight * (1.0 - part)
             cols = slice(half * BS, (half + 1) * BS)
             above = jnp.where(whole == 0.0, upper, 0.0)
+            hats = []
             for bin_at in range(NBIN):
                 here = whole == float(bin_at + 1)
-                spline[bin_at * PT : (bin_at + 1) * PT, cols] = jnp.where(here, lower, above).astype(
-                    jnp.bfloat16
-                )
+                hats.append(jnp.where(here, lower, above))
                 above = jnp.where(here, upper, 0.0)
+            for side in range(2):
+                part_rows = slice(side * 8, side * 8 + 8)
+                for bin_at in range(0, NBIN, 2):
+                    both = jnp.concatenate([hats[bin_at][part_rows], hats[bin_at + 1][part_rows]])
+                    at = side * 128 + bin_at * 8
+                    spline[at : at + 16, cols] = both.astype(jnp.bfloat16)
         angular = [[None, None], [None, None]]
         for orders in GROUPS:
             for half in range(2):
@@ -312,24 +311,28 @@
                                 basis[low : low + PT, cols] = value.astype(jnp.bfloat16)
             first = first_row(orders[0]) * PT
             last = NHARM * PT if orders[-1] == LMAX else first_row(orders[-1] + 1) * PT
-            acc[first:last, :] += lax.dot_general(
+            product = lax.dot_general(
                 basis[first:last, :],
                 spline[...],
                 (((1,), (1,)), ((), ())),
                 preferred_element_type=jnp.float32,
+            ).reshape(-1, 2, 8, 2 * BS)
+            wanted = jnp.concatenate(
+                [product[:, 0:1, :, 0:128], product[:, 1:2, :, 128:256]], axis=1
             )
+            acc[first:last, :] += wanted.reshape(last - first, 128)
         return carry
 
     lax.fori_loop(0, chunks, chunk_step, 0)
 
-    row = lax.broadcasted_iota(jnp.int32, (PT, PT * NBIN), 0)
-    col = lax.broadcasted_iota(jnp.int32, (PT, PT * NBIN), 1)
-    keep = jnp.where(col % PT == row, scale_column, 0.0)
+    row = lax.broadcasted_iota(jnp.int32, (PT, 128), 0)
+    col = lax.broadcasted_iota(jnp.int32, (PT, 128), 1)
+    keep = jnp.where((col & 7) == (row & 7), scale_column, 0.0)
     for harm in range(128):
         if harm < NHARM:
             value = (acc[harm * PT : (harm + 1) * PT, :] * keep).astype(jnp.bfloat16)
         else:
-            value = jnp.zeros((PT, PT * NBIN), jnp.bfloat16)
+            value = jnp.zeros((PT, 128), jnp.bfloat16)
         diag[harm % 8, (harm // 8) * PT : (harm // 8 + 1) * PT, :] = value
     total = jnp.zeros((256, 128), jnp.float32)
     for part in range(8):
@@ -338,13 +341,13 @@
     for group in range(15):
         coef_ref[:, group * 128 : (group + 1) * 128] = rows[group * PT : (group + 1) * PT, :]
     coef_ref[:, 1920:FEAT] = rows[15 * PT : 16 * PT, : FEAT - 1920]
-    turned = jnp.dot(turn_matrix(), rows, preferred_element_type=jnp.float32)
+    turned = jnp.dot(turn_ref[...], rows, preferred_element_type=jnp.float32)
     rows_ref[...] = turned.astype(jnp.bfloat16).reshape(PT, 16, 128)
 
 
-def pair_sums(lists, pool, live, codes, pos, weight):
+def pair_sums(lists, *operands):
     tiles = lists.shape[0]
-    operands = (pool, live, codes, pos, weight)
+    live = operands[1]
     return pl.pallas_call(
         pair_kernel,
         out_shape=(
@@ -355,7 +358,7 @@
         grid_spec=pltpu.PrefetchScalarGridSpec(
             num_scalar_prefetch=1,
             grid=(tiles,),
-            in_specs=[pl.BlockSpec(memory_space=pltpu.HBM)] * len(operands),
+            in_specs=[pl.BlockSpec(memory_space=pltpu.VMEM)] * len(operands),
             out_specs=(
                 pl.BlockSpec((PT, FEAT), lambda t, *_: (t, 0)),
                 pl.BlockSpec((PT, 16, 128), lambda t, *_: (t, 0, 0)),
@@ -365,15 +368,10 @@
                 pltpu.VMEM((2 * ((LIST + 1) // 2) + 2, 8, BS), jnp.float32),
                 pltpu.VMEM((NHARM * PT, 2 * BS), jnp.bfloat16),
                 pltpu.VMEM((NBIN * PT, 2 * BS), jnp.bfloat16),
-                pltpu.VMEM((NHARM * PT, NBIN * PT), jnp.float32),
-                pltpu.VMEM((8, 256, NBIN * PT), jnp.bfloat16),
-                pltpu.VMEM((8, NBIN * PT, 128), jnp.bfloat16),
-                pltpu.VMEM(pool.shape, pool.dtype),
+                pltpu.VMEM((NHARM * PT, 128), jnp.float32),
+                pltpu.VMEM((8, 256, 128), jnp.bfloat16),
                 pltpu.SMEM(live.shape, live.dtype),
-                pltpu.VMEM(codes.shape, codes.dtype),
-                pltpu.VMEM(pos.shape, pos.dtype),
-                pltpu.VMEM(weight.shape, weight.dtype),
-                pltpu.SemaphoreType.DMA((len(operands),)),
+                pltpu.SemaphoreType.DMA(()),
             ],
         ),
         compiler_params=pltpu.CompilerParams(vmem_limit_bytes=40 << 20),
@@ -617,11 +615,11 @@
 
 
 def shards(prim_pos, prim_weight, sec_pos, sec_weight, sec_counts, tile_lists, region_of):
-    pool, live, codes = near(
+    pool, live, codes, spread, turn = near(
         sec_counts, sec_pos.transpose(1, 0, 2), sec_weight, region_of.reshape(1, -1)
     )
     coefficients, rows, table = pair_sums(
-        tile_lists, pool, live, codes, prim_pos, prim_weight.reshape(1, -1)
+        tile_lists, pool, live, codes, prim_pos, prim_weight.reshape(1, -1), spread, turn
     )
     region_tensor = region_products(table, rows).reshape(1, -1)
     return (coefficients, region_tensor)

time: 75.2 us -> 74 us (0.984)
  Pallas kernels: 70.8 us -> 69.6 us
    pallas_call x1, Pallas kernels: 13.5 us -> 12 us  [pair_sums(): pl.pallas_call(pair_kernel, out_shape=(jax.ShapeDtypeStruct((tiles * PT,...]
where the time goes in v5:
time: 74 us; the launch traced here: 73.7 us
  Pallas kernels  69.6 us (94%)
  local copies, waits for them, and re-layouts  3.37 us (5%)
    pallas_call x1, Pallas kernels, region_products(): pl.pallas_call(regions_kernel, out_shape=jax.ShapeDtypeStruct((total // 1...  40.9 us
    pallas_call x1, Pallas kernels, near(): pl.pallas_call(near_kernel, out_shape=(jax.ShapeDtypeStruct((6, BLK_DEV,...  16.7 us
    pallas_call x1, Pallas kernels, pair_sums(): pl.pallas_call(pair_kernel, out_shape=(jax.ShapeDtypeStruct((tiles * PT,...  12 us
    unnamed x15, local copies, waits for them, and re-layouts  3.37 us

profile of v5, /device:TPU:1, one launch (start us, length us, event | category | flops | bytes accessed | tf_op | source)
XLA Modules:
  0.0 73.7 jit_solution(10832971842754912517)
XLA Ops:
  0.6 0.0 copy-start.1
  0.6 0.0 copy-start.4
  0.7 0.0 copy-start.5
  0.7 0.7 copy-done.1
  1.3 0.0 copy-done.4
  1.3 0.0 copy-done.5
  1.3 0.0 copy-start
  1.3 0.7 copy-done
  2.0 16.7 %near.1 = (f32[6,8,8,128]{3,2,1,0:T(8,128)S(1)}, s32[6,1,128]{2,1,0:T(1,128)S(1)}, s32[8,1,128]{2,1,0:T(1,128)S(1)}, bf16[8,128,128]{2,1,0:T(8,128)(2,1)S(1)}, bf16[256,256]{1,0:T(8,128)(2,1)S(1)}) custom-call(s32[8]{0:T(128)S(1)} %copy-done.4, f32[3,8,128]{2,1,0:T(8,128)S(1)} %bitcast.9, f32[8,128]{1,0:T(8,128)S(1)} %copy-done.1, s32[1,64]{1,0:T(1,128)S(1)} %bitcast.10), custom_call_target="tpu_custom_call" | custom-call | tf_op jit(solution)/shard_map/near/pallas_call | solution.py:161
  18.8 0.0 copy-start.3
  18.8 0.0 copy-start.2
  18.8 0.0 copy-start.6
  18.8 0.6 copy-done.3
  19.4 0.0 copy-done.2
  19.5 0.0 copy-done.6
  19.5 12.0 %pair_sums.1 = (bf16[64,1936]{1,0:T(8,128)(2,1)}, bf16[64,16,128]{2,1,0:T(8,128)(2,1)S(1)}, s32[64,128]{1,0:T(8,128)S(1)}) custom-call(s32[4,12]{1,0:T(4,128)S(1)} %copy-done.2, f32[6,8,8,128]{3,2,1,0:T(8,128)S(1)} %get-tuple-element.10.pool_ref, s32[6,1,128]{2,1,0:T(1,128)S(1)} %get-tuple-element.11.live_ref, s32[8,1,128]{2,1,0:T(1,128)S(1)} %get-tuple-element.12.code_ref, ...), custom_call_target="tpu_custom_call" | custom-call | tf_op jit(solution)/shard_map/pair_sums/pallas_call | solution.py:351
  31.5 40.9 %region_products.1 = f32[1012,128]{1,0:T(8,128)S(1)} custom-call(s32[64,128]{1,0:T(8,128)S(1)} %get-tuple-element.16.table_ref, bf16[64,16,128]{2,1,0:T(8,128)(2,1)S(1)} %get-tuple-element.17.rows_ref), custom_call_target="tpu_custom_call" | custom-call | tf_op jit(solution)/shard_map/region_products/pallas_call | solution.py:588
  72.4 1.3 %copy.11 = f32[1,1,1012,128]{3,1,2,0:T(1,128)} copy(f32[1,1,1012,128]{3,2,1,0:T(8,128)S(1)} %bitcast.8) | data formatting | bytes 1036288
Async XLA Ops:
  0.6 0.7 copy-start.1
  0.6 0.7 copy-start.4
  0.7 0.7 copy-start.5
  1.3 0.7 copy-start
  18.8 0.7 copy-start.3
  18.8 0.7 copy-start.2
  18.8 0.7 copy-start.6

commit v6 on v5

--- a/solution.py
+++ b/solution.py
@@ -92,7 +92,6 @@
         for axis in range(3):
             pool_ref[mine, block, axis : axis + 1, :] = pos_ref[axis, block : block + 1, :]
         pool_ref[mine, block, 3:4, :] = jnp.where(lane < count, weight_ref[block : block + 1, :], 0.0)
-        pool_ref[mine, block, 4:8, :] = jnp.zeros((4, BS), jnp.float32)
     live_ref[mine] = live
     row = lax.broadcasted_iota(jnp.int32, (PRIM_DEV, BS), 0)
     col = lax.broadcasted_iota(jnp.int32, (PRIM_DEV, BS), 1)
@@ -103,65 +102,38 @@
 
     pl.semaphore_wait(barrier, 12)
 
-    def block_copy(slot, kind, target):
-        ref = (pool_ref, live_ref)[kind]
-        return pltpu.make_async_remote_copy(
-            src_ref=ref.at[mine],
-            dst_ref=ref.at[slot],
-            send_sem=send.at[slot, kind],
-            recv_sem=recv.at[slot, kind],
+    def push(kind, ref, from_at, to_at, target):
+        pltpu.make_async_remote_copy(
+            src_ref=ref.at[from_at],
+            dst_ref=ref.at[to_at],
+            send_sem=send.at[kind],
+            recv_sem=recv.at[kind],
             device_id=target,
             device_id_type=MESH,
-        )
-
-    def code_copy(z_from, step):
-        return pltpu.make_async_remote_copy(
-            src_ref=code_ref.at[z_from],
-            dst_ref=code_ref.at[z_from],
-            send_sem=send.at[5 + step, 0],
-            recv_sem=recv.at[6 + z_from, 0],
-            device_id=line[step - 1],
-            device_id_type=MESH,
-        )
-
-    sends = []
-    for at, (to_box, to_core, move) in enumerate(near):
-        for kind in range(2):
-            ref = (pool_ref, live_ref)[kind]
-            sends.append(
-                pltpu.make_async_remote_copy(
-                    src_ref=ref.at[mine],
-                    dst_ref=ref.at[2 * move + core],
-                    send_sem=send.at[at, kind],
-                    recv_sem=recv.at[2 * move + core, kind],
-                    device_id=(to_box, to_core),
-                    device_id_type=MESH,
-                )
-            )
-    for step in range(1, Z_SIZE):
-        sends.append(code_copy(z_at, step))
-    for copy in sends:
-        copy.start()
+        ).start()
+
+    for step in (4, 3, 5, 2, 6, 1, 7):
+        push(2, code_ref, z_at, z_at, line[step - 1])
+    for to_box, to_core, move in near:
+        push(0, pool_ref, mine, 2 * move + core, (to_box, to_core))
+        push(1, live_ref, mine, 2 * move + core, (to_box, to_core))
     row = lax.broadcasted_iota(jnp.int32, (128, 128), 0)
     col = lax.broadcasted_iota(jnp.int32, (128, 128), 1)
     for part in range(8):
         hit = col - part * NBIN == row // 8
         spread_ref[part] = jnp.where(hit, 1.0, 0.0).astype(jnp.bfloat16)
     turn_ref[...] = turn_matrix()
-    for slot in (0, 1, 4, 5, 2 + other):
-        for kind in range(2):
-            block_copy(slot, kind, (box, other)).wait_recv()
-    for step in range(1, Z_SIZE):
-        code_copy((z_at + step) % Z_SIZE, step).wait_recv()
-    for copy in sends:
-        copy.wait_send()
+    for sems in (recv, send):
+        for kind, (ref, number) in enumerate(((pool_ref, 5), (live_ref, 5), (code_ref, 7))):
+            moved = ref.at[pl.ds(0, number)]
+            pltpu.make_async_copy(moved, moved, sems.at[kind]).wait()
 
 
 def near(counts, pos, weight, regions):
     return pl.pallas_call(
         near_kernel,
         out_shape=(
-            jax.ShapeDtypeStruct((6, BLK_DEV, 8, BS), jnp.float32),
+            jax.ShapeDtypeStruct((6, BLK_DEV, 4, BS), jnp.float32),
             jax.ShapeDtypeStruct((6, 1, BS), jnp.int32),
             jax.ShapeDtypeStruct((Z_SIZE, 1, BS), jnp.int32),
             jax.ShapeDtypeStruct((8, 128, 128), jnp.bfloat16),
@@ -170,7 +142,7 @@
         in_specs=[pl.BlockSpec(memory_space=pltpu.SMEM)]
         + [pl.BlockSpec(memory_space=pltpu.VMEM)] * 3,
         out_specs=(pl.BlockSpec(memory_space=pltpu.VMEM),) * 5,
-        scratch_shapes=[pltpu.SemaphoreType.DMA((13, 2)), pltpu.SemaphoreType.DMA((14, 2))],
+        scratch_shapes=[pltpu.SemaphoreType.DMA((3,)), pltpu.SemaphoreType.DMA((3,))],
         compiler_params=pltpu.CompilerParams(
             collective_id=0, has_side_effects=True, vmem_limit_bytes=8 << 20
         ),
@@ -184,7 +156,7 @@
 ):
     tile = pl.program_id(0)
     box, core = lax.axis_index("box"), lax.axis_index("help")
-    lane = lax.broadcasted_iota(jnp.int32, (8, BS), 1)
+    lane = lax.broadcasted_iota(jnp.int32, (4, BS), 1)
 
     @pl.when(tile == 0)
     def _():
@@ -365,7 +337,7 @@
                 pl.BlockSpec((2 * PEERS, BS), lambda t, *_: (0, 0)),
             ),
             scratch_shapes=[
-                pltpu.VMEM((2 * ((LIST + 1) // 2) + 2, 8, BS), jnp.float32),
+                pltpu.VMEM((2 * ((LIST + 1) // 2) + 2, 4, BS), jnp.float32),
                 pltpu.VMEM((NHARM * PT, 2 * BS), jnp.bfloat16),
                 pltpu.VMEM((NBIN * PT, 2 * BS), jnp.bfloat16),
                 pltpu.VMEM((NHARM * PT, 128), jnp.float32),
@@ -410,8 +382,8 @@
 
 
 PLANE_MOVES = (
-    (1, 0), (3, 0), (0, 1), (0, 3), (1, 1), (3, 3), (1, 3), (3, 1),
-    (2, 0), (0, 2), (2, 2), (2, 1), (1, 2), (2, 3), (3, 2),
+    (2, 2), (2, 1), (1, 2), (2, 3), (3, 2), (1, 1), (3, 3), (1, 3),
+    (3, 1), (2, 0), (0, 2), (1, 0), (3, 0), (0, 1), (0, 3),
 )
 BATCHES = ((0, 1), (1, 2), (3, 2), (5, 2), (7, 1))
 
@@ -532,10 +504,11 @@
             plain[tile, at : at + size, :] = down.astype(jnp.bfloat16)
             flipped[tile, :, at : at + size] = over.astype(jnp.bfloat16)
 
-    for half in range(2):
-        for way in range(2):
-            ring_copy(way, 1, half).start()
+    for way in range(2):
+        ring_copy(way, 1, 0).start()
     deal(0)
+    for way in range(2):
+        ring_copy(way, 1, 1).start()
     prepare()
     for step in range(1, 4):
         for half in range(2):

time: 74 us -> 71.6 us (0.968)
  Pallas kernels: 69.6 us -> 67.3 us
    pallas_call x1, Pallas kernels: 40.9 us -> 39.9 us  [region_products(): pl.pallas_call(regions_kernel, out_shape=jax.ShapeDtypeStruct((total // 1...]
    pallas_call x1, Pallas kernels: 16.7 us -> 16 us  [near(): pl.pallas_call(near_kernel, out_shape=(jax.ShapeDtypeStruct((6, BLK_DEV,...]
where the time goes in v6:
time: 71.6 us; the launch traced here: 71.4 us
  Pallas kernels  67.3 us (94%)
  local copies, waits for them, and re-layouts  3.37 us (5%)
    pallas_call x1, Pallas kernels, region_products(): pl.pallas_call(regions_kernel, out_shape=jax.ShapeDtypeStruct((total // 1...  39.9 us
    pallas_call x1, Pallas kernels, near(): pl.pallas_call(near_kernel, out_shape=(jax.ShapeDtypeStruct((6, BLK_DEV,...  16 us
    pallas_call x1, Pallas kernels, pair_sums(): pl.pallas_call(pair_kernel, out_shape=(jax.ShapeDtypeStruct((tiles * PT,...  11.5 us
    unnamed x15, local copies, waits for them, and re-layouts  3.37 us

profile of v6, /device:TPU:1, one launch (start us, length us, event | category | flops | bytes accessed | tf_op | source)
XLA Modules:
  0.0 71.4 jit_solution(7485613681579019297)
XLA Ops:
  0.6 0.0 copy-start.1
  0.6 0.0 copy-start.5
  0.7 0.0 copy-start.6
  0.7 0.7 copy-done.1
  1.3 0.0 copy-done.5
  1.3 0.0 copy-done.6
  1.3 0.0 copy-start
  1.3 0.7 copy-done
  2.0 16.0 %near.1 = (f32[6,8,4,128]{3,2,1,0:T(4,128)S(1)}, s32[6,1,128]{2,1,0:T(1,128)S(1)}, s32[8,1,128]{2,1,0:T(1,128)S(1)}, bf16[8,128,128]{2,1,0:T(8,128)(2,1)S(1)}, bf16[256,256]{1,0:T(8,128)(2,1)S(1)}) custom-call(s32[8]{0:T(128)S(1)} %copy-done.5, f32[3,8,128]{2,1,0:T(8,128)S(1)} %bitcast.9, f32[8,128]{1,0:T(8,128)S(1)} %copy-done.1, s32[1,64]{1,0:T(1,128)S(1)} %bitcast.11), custom_call_target="tpu_custom_call" | custom-call | tf_op jit(solution)/shard_map/near/pallas_call | solution.py:133
  18.0 0.0 copy-start.3
  18.0 0.0 copy-start.2
  18.0 0.0 copy-start.4
  18.0 0.6 copy-done.3
  18.7 0.0 copy-done.2
  18.7 0.0 copy-done.4
  18.7 11.5 %pair_sums.1 = (bf16[64,1936]{1,0:T(8,128)(2,1)}, bf16[64,16,128]{2,1,0:T(8,128)(2,1)S(1)}, s32[64,128]{1,0:T(8,128)S(1)}) custom-call(s32[4,12]{1,0:T(4,128)S(1)} %copy-done.2, f32[6,8,4,128]{3,2,1,0:T(4,128)S(1)} %get-tuple-element.10.pool_ref, s32[6,1,128]{2,1,0:T(1,128)S(1)} %get-tuple-element.11.live_ref, s32[8,1,128]{2,1,0:T(1,128)S(1)} %get-tuple-element.12.code_ref, ...), custom_call_target="tpu_custom_call" | custom-call | tf_op jit(solution)/shard_map/pair_sums/pallas_call | solution.py:323
  30.2 39.9 %region_products.1 = f32[1012,128]{1,0:T(8,128)S(1)} custom-call(s32[64,128]{1,0:T(8,128)S(1)} %get-tuple-element.16.table_ref, bf16[64,16,128]{2,1,0:T(8,128)(2,1)S(1)} %get-tuple-element.17.rows_ref), custom_call_target="tpu_custom_call" | custom-call | tf_op jit(solution)/shard_map/region_products/pallas_call | solution.py:561
  70.1 1.3 %copy.11 = f32[1,1,1012,128]{3,1,2,0:T(1,128)} copy(f32[1,1,1012,128]{3,2,1,0:T(8,128)S(1)} %bitcast.8) | data formatting | bytes 1036288
Async XLA Ops:
  0.6 0.7 copy-start.1
  0.6 0.7 copy-start.5
  0.7 0.7 copy-start.6
  1.3 0.7 copy-start
  18.0 0.7 copy-start.3
  18.0 0.7 copy-start.2
  18.0 0.7 copy-start.4

commit v7 on v6

--- a/solution.py
+++ b/solution.py
@@ -56,6 +56,14 @@
     for step in range(m_order + 1, degree + 1):
         lead = lead * (2 * step - 1) / (step - m_order)
     return factor * lead
+
+
+def harmonic_scales():
+    scales = []
+    for m_order in range(LMAX + 1):
+        row = [harmonic_scale(m_order, degree) for degree in range(m_order, LMAX + 1)]
+        scales += row if m_order == 0 else row + row
+    return scales
 
 
 def first_row(m_order):
@@ -266,19 +274,14 @@
                             else:
                                 current = uz * newer - ratio * older
                         older, newer = newer, current
-                        scale = harmonic_scale(m_order, degree)
                         at = (start + degree - m_order) * PT
-                        if current is None:
-                            scaled = None
-                        else:
-                            scaled = current * scale
                         if m_order == 0:
-                            value = jnp.full((PT, BS), scale, jnp.float32) if scaled is None else scaled
+                            value = jnp.ones((PT, BS), jnp.float32) if current is None else current
                             basis[at : at + PT, cols] = value.astype(jnp.bfloat16)
                         else:
                             for kind in range(2):
                                 turn = angular[half][kind]
-                                value = turn * scale if scaled is None else scaled * turn
+                                value = turn if current is None else current * turn
                                 low = at + kind * count * PT
                                 basis[low : low + PT, cols] = value.astype(jnp.bfloat16)
             first = first_row(orders[0]) * PT
@@ -300,9 +303,11 @@
     row = lax.broadcasted_iota(jnp.int32, (PT, 128), 0)
     col = lax.broadcasted_iota(jnp.int32, (PT, 128), 1)
     keep = jnp.where((col & 7) == (row & 7), scale_column, 0.0)
+    scales = harmonic_scales()
     for harm in range(128):
         if harm < NHARM:
-            value = (acc[harm * PT : (harm + 1) * PT, :] * keep).astype(jnp.bfloat16)
+            value = acc[harm * PT : (harm + 1) * PT, :] * (keep * scales[harm])
+            value = value.astype(jnp.bfloat16)
         else:
             value = jnp.zeros((PT, 128), jnp.bfloat16)
         diag[harm % 8, (harm // 8) * PT : (harm // 8 + 1) * PT, :] = value

time: 71.6 us -> 71.3 us (level)
  Pallas kernels: 67.3 us -> 66.5 us
    pallas_call x1, Pallas kernels: 39.9 us -> 38.9 us  [region_products(): pl.pallas_call(regions_kernel, out_shape=jax.ShapeDtypeStruct((total // 1...]
where the time goes in v7:
time: 71.3 us; the launch traced here: 70.5 us
  Pallas kernels  66.5 us (93%)
  local copies, waits for them, and re-layouts  3.37 us (5%)
    pallas_call x1, Pallas kernels, region_products(): pl.pallas_call(regions_kernel, out_shape=jax.ShapeDtypeStruct((total // 1...  38.9 us
    pallas_call x1, Pallas kernels, near(): pl.pallas_call(near_kernel, out_shape=(jax.ShapeDtypeStruct((6, BLK_DEV,...  16 us
    pallas_call x1, Pallas kernels, pair_sums(): pl.pallas_call(pair_kernel, out_shape=(jax.ShapeDtypeStruct((tiles * PT,...  11.6 us
    unnamed x15, local copies, waits for them, and re-layouts  3.37 us

profile of v7, /device:TPU:1, one launch (start us, length us, event | category | flops | bytes accessed | tf_op | source)
XLA Modules:
  0.0 70.5 jit_solution(1450975990559514356)
XLA Ops:
  0.6 0.0 copy-start.1
  0.6 0.0 copy-start.5
  0.7 0.0 copy-start.6
  0.7 0.7 copy-done.1
  1.3 0.0 copy-done.5
  1.3 0.0 copy-done.6
  1.3 0.0 copy-start
  1.3 0.7 %copy-done = f32[8,3,128]{2,0,1:T(8,128)S(1)} copy-done((f32[8,3,128]{2,0,1:T(8,128)S(1)}, f32[8,3,128]{2,0,1:T(8,128)}, u32[]{:S(2)}) %copy-start) | copy-done | bytes 12312
  2.0 16.0 %near.1 = (f32[6,8,4,128]{3,2,1,0:T(4,128)S(1)}, s32[6,1,128]{2,1,0:T(1,128)S(1)}, s32[8,1,128]{2,1,0:T(1,128)S(1)}, bf16[8,128,128]{2,1,0:T(8,128)(2,1)S(1)}, bf16[256,256]{1,0:T(8,128)(2,1)S(1)}) custom-call(s32[8]{0:T(128)S(1)} %copy-done.5, f32[3,8,128]{2,1,0:T(8,128)S(1)} %bitcast.9, f32[8,128]{1,0:T(8,128)S(1)} %copy-done.1, s32[1,64]{1,0:T(1,128)S(1)} %bitcast.11), custom_call_target="tpu_custom_call" | custom-call | tf_op jit(solution)/shard_map/near/pallas_call | solution.py:141
  18.0 0.0 copy-start.3
  18.0 0.0 copy-start.2
  18.0 0.0 copy-start.4
  18.0 0.6 copy-done.3
  18.7 0.0 copy-done.2
  18.7 0.0 copy-done.4
  18.7 11.6 %pair_sums.1 = (bf16[64,1936]{1,0:T(8,128)(2,1)}, bf16[64,16,128]{2,1,0:T(8,128)(2,1)S(1)}, s32[64,128]{1,0:T(8,128)S(1)}) custom-call(s32[4,12]{1,0:T(4,128)S(1)} %copy-done.2, f32[6,8,4,128]{3,2,1,0:T(4,128)S(1)} %get-tuple-element.10.pool_ref, s32[6,1,128]{2,1,0:T(1,128)S(1)} %get-tuple-element.11.live_ref, s32[8,1,128]{2,1,0:T(1,128)S(1)} %get-tuple-element.12.code_ref, ...), custom_call_target="tpu_custom_call" | custom-call | tf_op jit(solution)/shard_map/pair_sums/pallas_call | solution.py:328
  30.3 38.9 %region_products.1 = f32[1012,128]{1,0:T(8,128)S(1)} custom-call(s32[64,128]{1,0:T(8,128)S(1)} %get-tuple-element.16.table_ref, bf16[64,16,128]{2,1,0:T(8,128)(2,1)S(1)} %get-tuple-element.17.rows_ref), custom_call_target="tpu_custom_call" | custom-call | tf_op jit(solution)/shard_map/region_products/pallas_call | solution.py:566
  69.2 1.3 %copy.11 = f32[1,1,1012,128]{3,1,2,0:T(1,128)} copy(f32[1,1,1012,128]{3,2,1,0:T(8,128)S(1)} %bitcast.8) | data formatting | bytes 1036288
Async XLA Ops:
  0.6 0.7 copy-start.1
  0.6 0.7 copy-start.5
  0.7 0.7 copy-start.6
  1.3 0.7 %copy-start = (f32[8,3,128]{2,0,1:T(8,128)S(1)}, f32[8,3,128]{2,0,1:T(8,128)}, u32[]{:S(2)}) copy-start(f32[8,3,128]{2,0,1:T(8,128)} %param.9) | copy-start | bytes 36868
  18.0 0.7 copy-start.3
  18.0 0.7 copy-start.2
  18.0 0.7 copy-start.4
